TPU v7x, 32 devices: a whole 2x2x4 slice. The times are simulated.
32 devices in a mesh: gx: 4 (over y, core), gy: 8 (over z, x).
Axes of the slice: x: 2, y: 2, z: 4, core: 2. Of those that a mesh axis runs over, the one named last changes fastest.
Arguments:
- hidden_in: bfloat16 [3072, 2304], P('gy', 'gx'), may hold values from -6 to 6
- out_grad: bfloat16 [3072, 2304], P('gy', 'gx'), may hold values from -6 to 6
- seq_ids: int32 [3072], replicated, may hold values from 0 to 2, never falling along the last dimension, each value on 1 to 2048 neighbouring positions
- qkv_weight: bfloat16 [2304, 4, 1024], P('gy', 'gx'), may hold values from -0.25 to 0.25
- out_weight: bfloat16 [2048, 2304], P('gx', 'gy'), may hold values from -0.75 to 0.75
- gate_up_weight: bfloat16 [2304, 2, 9216], P('gy', None, 'gx'), may hold values from -0.125 to 0.125
- down_weight: bfloat16 [9216, 2304], P('gx', 'gy'), may hold values from -0.0625 to 0.0625
- norm_gains: bfloat16 [4, 2304], P(None, 'gy'), may hold values from -0.59765625 to 0.59765625
- moment_qkv: float32 [2304, 4, 1024], P('gy', 'gx'), may hold values from -112 to 112
- moment_out: float32 [2048, 2304], P('gx', 'gy'), may hold values from -10 to 10
- moment_gate_up: float32 [2304, 2, 9216], P('gy', None, 'gx'), may hold values from -16 to 16
- moment_down: float32 [9216, 2304], P('gx', 'gy'), may hold values from -32 to 32
- moment_gains: float32 [4, 2304], P(None, 'gy'), may hold values from -56 to 56
- square_qkv: float32 [2304, 4, 1024], P('gy', 'gx'), may hold values from 768 to 3072
- square_out: float32 [2048, 2304], P('gx', 'gy'), may hold values from 7.68 to 30.72
- square_gate_up: float32 [2304, 2, 9216], P('gy', None, 'gx'), may hold values from 21.504 to 82.944
- square_down: float32 [9216, 2304], P('gx', 'gy'), may hold values from 82.944 to 307.2
- square_gains: float32 [4, 2304], P(None, 'gy'), may hold values from 184.32 to 737.28
Outputs:
- block_out: bfloat16 [3072, 2304], P('gy', 'gx')
- input_grad: float32 [3072, 2304], P('gy', 'gx')
- grad_qkv: float32 [2304, 4, 1024], P('gy', 'gx')
- grad_out: float32 [2048, 2304], P('gx', 'gy')
- grad_gate_up: float32 [2304, 2, 9216], P('gy', None, 'gx')
- grad_down: float32 [9216, 2304], P('gx', 'gy')
- grad_gains: float32 [4, 2304], P(None, 'gy')
- moment_qkv_new: float32 [2304, 4, 1024], P('gy', 'gx')
- moment_out_new: float32 [2048, 2304], P('gx', 'gy')
- moment_gate_up_new: float32 [2304, 2, 9216], P('gy', None, 'gx')
- moment_down_new: float32 [9216, 2304], P('gx', 'gy')
- moment_gains_new: float32 [4, 2304], P(None, 'gy')
- square_qkv_new: float32 [2304, 4, 1024], P('gy', 'gx')
- square_out_new: float32 [2048, 2304], P('gx', 'gy')
- square_gate_up_new: float32 [2304, 2, 9216], P('gy', None, 'gx')
- square_down_new: float32 [9216, 2304], P('gx', 'gy')
- square_gains_new: float32 [4, 2304], P(None, 'gy')
- update_qkv: float32 [2304, 4, 1024], P('gy', 'gx')
- update_out: float32 [2048, 2304], P('gx', 'gy')
- update_gate_up: float32 [2304, 2, 9216], P('gy', None, 'gx')
- update_down: float32 [9216, 2304], P('gx', 'gy')
- update_gains: float32 [4, 2304], P(None, 'gy')
Inputs may be any that keep to these rules, and one draw needn't show every extreme that they name: `seq_ids`: sequence numbers never fall along the tokens; every sequence has 1 to 2048 tokens, and one has exactly 2048.
All inputs are finite; a program needn't handle non-finite values.
Results may differ from a plain program's by a relative error of at most 0.03.
The roundings to bfloat16 on the way count: a program that leaves them out, or rounds other values in their place, can miss the bound.
Values may be sent and summed in bfloat16 or wider, within the bound.
No kernel may reach another device: no remote copies, remote signals or barrier semaphores. Data moves between devices by JAX's collectives and lax.ppermute only.
A program may use at most 320 MiB of HBM per device.

v0:
```python
import math

import jax
import jax.numpy as jnp
from jax import lax
from jax.sharding import PartitionSpec as P

HEADS = 8
KV = 4
HEAD = 256
MEAN_LEN = 1024


NORM_EPS = 1e-06
SOFT_CAP = 50.0
MASKED_SCORE = -1e30
BETA_ONE = 0.9
BETA_TWO = 0.95
FIRST_FIX = 1.0 - 0.9**10
SECOND_FIX = 1.0 - 0.95**10
LEARN_RATE = 0.05
WEIGHT_DECAY = 0.1
ADAM_EPS = 1e-08


def shifted(block, axis, distance):
    devices = range(lax.axis_size(axis))
    route = [(i - distance, i) for i in devices if i - distance in devices]
    return lax.ppermute(block, axis, route)


def rms_norm(values, gain_row):
    return (
        values
        * lax.rsqrt(jnp.mean(values * values, axis=-1, keepdims=True) + NORM_EPS)
        * (1.0 + gain_row)
    )


def rotate(tensor, cosine, sine_part):
    half_dim = tensor.shape[-1] // 2
    leading = tensor[..., :half_dim]
    trailing = tensor[..., half_dim:]
    return jnp.concatenate(
        [leading * cosine - trailing * sine_part, trailing * cosine + leading * sine_part], axis=-1
    )


def geglu_mix(gate_pre, up_pre):
    return jax.nn.gelu(gate_pre, approximate=True) * up_pre


def adamw_step(weight, gradient, moment, square):
    weight_wide = weight.astype(jnp.float32)
    moment_new = BETA_ONE * moment + (1.0 - BETA_ONE) * gradient
    square_new = BETA_TWO * square + (1.0 - BETA_TWO) * gradient * gradient
    update = -LEARN_RATE * (
        moment_new / FIRST_FIX / (jnp.sqrt(square_new / SECOND_FIX) + ADAM_EPS)
        + WEIGHT_DECAY * weight_wide
    )
    return (moment_new, square_new, update)


def capped_scores(query_rot, key_part, allowed):
    raw_scores = jnp.einsum(
        "qkgd,skd->kgqs", query_rot, key_part, preferred_element_type=jnp.float32
    )
    bent_raw = jnp.tanh(raw_scores / SOFT_CAP)
    return (bent_raw, jnp.where(allowed, SOFT_CAP * bent_raw, MASKED_SCORE))


def local(
    hidden_in,
    out_grad,
    seq_ids,
    qkv_weight,
    out_weight,
    gate_up_weight,
    down_weight,
    norm_gains,
    moment_qkv,
    moment_out,
    moment_gate_up,
    moment_down,
    moment_gains,
    square_qkv,
    square_out,
    square_gate_up,
    square_down,
    square_gains,
):
    rows_here = hidden_in.shape[0]
    feat_share = hidden_in.shape[1]
    local_kv = qkv_weight.shape[1]
    group_size = HEADS // KV
    gy_count = lax.axis_size("gy")
    gy_index = lax.axis_index("gy")
    gx_index = lax.axis_index("gx")
    reach_back = min((2 * MEAN_LEN - 2) // rows_here + 1, gy_count - 1)
    hidden_all, grad_all = (
        lax.all_gather(hidden_in, "gx", axis=1, tiled=True),
        lax.all_gather(out_grad, "gx", axis=1, tiled=True),
    )
    qkv_all, out_all, gains_all = (
        lax.all_gather(qkv_weight, "gy", axis=0, tiled=True),
        lax.all_gather(out_weight, "gy", axis=1, tiled=True),
        lax.all_gather(norm_gains, "gy", axis=1, tiled=True),
    )
    gate_up_all, down_all = (
        lax.all_gather(gate_up_weight, "gy", axis=0, tiled=True),
        lax.all_gather(down_weight, "gy", axis=1, tiled=True),
    )
    gains_wide = gains_all.astype(jnp.float32)
    hidden_wide = hidden_all.astype(jnp.float32)
    first_row = gy_index * rows_here
    query_index = first_row + jnp.arange(rows_here, dtype=jnp.int32)
    inverse = jnp.exp(jnp.arange(HEAD // 2, dtype=jnp.float32) * (-2.0 * math.log(10000.0) / HEAD))
    angles = query_index.astype(jnp.float32)[:, None] * inverse[None, :]
    cosine = jnp.cos(angles)
    sine_part = jnp.sin(angles)
    cos_query = cosine[:, None, None, :]
    sin_query = sine_part[:, None, None, :]
    cos_key = cosine[:, None, :]
    sin_key = sine_part[:, None, :]
    query_scale = HEAD ** (-0.5)
    normed_one, norm_one_back = jax.vjp(rms_norm, hidden_wide, gains_wide[0])
    normed_one = normed_one.astype(jnp.bfloat16)
    projected = jnp.einsum("td,dkc->tkc", normed_one, qkv_all, preferred_element_type=jnp.float32)
    query_raw = projected[:, :, : group_size * HEAD].reshape(rows_here, local_kv, group_size, HEAD)
    key_raw = projected[:, :, group_size * HEAD : (group_size + 1) * HEAD]
    value_raw = projected[:, :, (group_size + 1) * HEAD :]
    query_rot = (rotate(query_raw, cos_query, sin_query) * query_scale).astype(jnp.bfloat16)
    key_rot = rotate(key_raw, cos_key, sin_key).astype(jnp.bfloat16)
    key_value = jnp.concatenate([key_rot, value_raw.astype(jnp.bfloat16)], axis=-1)
    kv_blocks = [key_value]
    for offset in range(1, reach_back + 1):
        kv_blocks.append(shifted(key_value, "gy", offset))
    key_value_all = jnp.concatenate(kv_blocks, axis=0)
    key_index = jnp.concatenate(
        [
            (gy_index - offset) * rows_here + jnp.arange(rows_here, dtype=jnp.int32)
            for offset in range(reach_back + 1)
        ]
    )
    key_seq = jnp.concatenate(
        [
            lax.dynamic_slice_in_dim(
                seq_ids, jnp.maximum((gy_index - offset) * rows_here, 0), rows_here, 0
            )
            for offset in range(reach_back + 1)
        ]
    )
    query_seq = lax.dynamic_slice_in_dim(seq_ids, first_row, rows_here, 0)
    allowed = (
        (key_index[None, :] >= 0)
        & (key_index[None, :] <= query_index[:, None])
        & (key_seq[None, :] == query_seq[:, None])
    )
    key_part = key_value_all[..., :HEAD]
    value_part = key_value_all[..., HEAD:]
    bent_raw, scores = capped_scores(query_rot, key_part, allowed)
    row_top = jnp.max(scores, axis=-1, keepdims=True)
    exp_scores = jnp.exp(scores - row_top)
    row_total = jnp.sum(exp_scores, axis=-1, keepdims=True)
    attn_probs = exp_scores / row_total
    log_total = row_top + jnp.log(row_total)
    attended = jnp.einsum(
        "kgqs,skd->qkgd",
        attn_probs.astype(jnp.bfloat16),
        value_part,
        preferred_element_type=jnp.float32,
    )
    attn_low = attended.astype(jnp.bfloat16).reshape(rows_here, local_kv * group_size * HEAD)
    mixed_sum = lax.psum(jnp.dot(attn_low, out_all, preferred_element_type=jnp.float32), "gx")
    branch_one, post_one_back = jax.vjp(rms_norm, mixed_sum, gains_wide[1])
    resid_sum = hidden_wide + branch_one
    normed_two, norm_two_back = jax.vjp(rms_norm, resid_sum, gains_wide[2])
    normed_two = normed_two.astype(jnp.bfloat16)
    gate_up_val = jnp.einsum(
        "td,dcf->tcf", normed_two, gate_up_all, preferred_element_type=jnp.float32
    )
    hidden_act, geglu_back = jax.vjp(geglu_mix, gate_up_val[:, 0], gate_up_val[:, 1])
    hidden_act = hidden_act.astype(jnp.bfloat16)
    down_sum = lax.psum(jnp.dot(hidden_act, down_all, preferred_element_type=jnp.float32), "gx")
    branch_two, post_two_back = jax.vjp(rms_norm, down_sum, gains_wide[3])
    block_full = resid_sum + branch_two
    block_out = lax.dynamic_slice_in_dim(block_full, gx_index * feat_share, feat_share, 1).astype(
        jnp.bfloat16
    )
    qkv_all, out_all = (
        lax.all_gather(qkv_weight, "gy", axis=0, tiled=True),
        lax.all_gather(out_weight, "gy", axis=1, tiled=True),
    )
    gate_up_all, down_all = (
        lax.all_gather(gate_up_weight, "gy", axis=0, tiled=True),
        lax.all_gather(down_weight, "gy", axis=1, tiled=True),
    )
    grad_wide = grad_all.astype(jnp.float32)
    down_grad, gain_three = post_two_back(grad_wide)
    down_low = down_grad.astype(jnp.bfloat16)
    act_grad = jnp.einsum("td,fd->tf", down_low, down_all, preferred_element_type=jnp.float32)
    down_weight_grad = jnp.einsum(
        "tf,td->fd", hidden_act, down_low, preferred_element_type=jnp.float32
    )
    gate_grad, up_grad = geglu_back(act_grad)
    both_low = jnp.stack([gate_grad, up_grad], axis=1).astype(jnp.bfloat16)
    gate_up_weight_grad = jnp.einsum(
        "td,tcf->dcf", normed_two, both_low, preferred_element_type=jnp.float32
    )
    grad_gate_up, grad_down = (
        lax.psum_scatter(
            gate_up_weight_grad.astype(jnp.bfloat16), "gy", scatter_dimension=0, tiled=True
        ).astype(jnp.float32),
        lax.psum_scatter(
            down_weight_grad.astype(jnp.bfloat16), "gy", scatter_dimension=1, tiled=True
        ).astype(jnp.float32),
    )
    normed_two_grad = lax.psum(
        jnp.einsum("tcf,dcf->td", both_low, gate_up_all, preferred_element_type=jnp.float32), "gx"
    )
    resid_part, gain_two = norm_two_back(normed_two_grad)
    resid_grad = grad_wide + resid_part
    mixed_grad, gain_one = post_one_back(resid_grad)
    mixed_low = mixed_grad.astype(jnp.bfloat16)
    attn_grad = jnp.einsum(
        "td,cd->tc", mixed_low, out_all, preferred_element_type=jnp.float32
    ).astype(jnp.bfloat16)
    attn_grad = attn_grad.reshape(rows_here, local_kv, group_size, HEAD)
    out_weight_grad = jnp.einsum(
        "tc,td->cd", attn_low, mixed_low, preferred_element_type=jnp.float32
    )
    bent_raw, scores = capped_scores(query_rot, key_part, allowed)
    attn_probs = jnp.exp(scores - log_total)
    prob_grad = jnp.einsum(
        "qkgd,skd->kgqs", attn_grad, value_part, preferred_element_type=jnp.float32
    )
    row_delta = jnp.sum(attn_probs * prob_grad, axis=-1, keepdims=True)
    raw_grad = (attn_probs * (prob_grad - row_delta) * (1.0 - bent_raw * bent_raw)).astype(
        jnp.bfloat16
    )
    query_grad = jnp.einsum(
        "kgqs,skd->qkgd", raw_grad, key_part, preferred_element_type=jnp.float32
    )
    key_value_grad = jnp.concatenate(
        [
            jnp.einsum("kgqs,qkgd->skd", raw_grad, query_rot, preferred_element_type=jnp.float32),
            jnp.einsum(
                "kgqs,qkgd->skd",
                attn_probs.astype(jnp.bfloat16),
                attn_grad,
                preferred_element_type=jnp.float32,
            ),
        ],
        axis=-1,
    )
    kv_grad_mine = key_value_grad[:rows_here]
    for offset in range(1, reach_back + 1):
        kv_grad_mine = kv_grad_mine + shifted(
            key_value_grad[offset * rows_here : (offset + 1) * rows_here].astype(jnp.bfloat16),
            "gy",
            -offset,
        ).astype(jnp.float32)
    key_grad = rotate(kv_grad_mine[..., :HEAD], cos_key, -sin_key)
    value_grad = kv_grad_mine[..., HEAD:]
    query_raw_grad = rotate(query_grad * query_scale, cos_query, -sin_query).reshape(
        rows_here, local_kv, group_size * HEAD
    )
    projected_low = jnp.concatenate([query_raw_grad, key_grad, value_grad], axis=-1).astype(
        jnp.bfloat16
    )
    qkv_weight_grad = jnp.einsum(
        "td,tkc->dkc", normed_one, projected_low, preferred_element_type=jnp.float32
    )
    normed_one_grad = lax.psum(
        jnp.einsum(
            "tkc,dkc->td", projected_low, qkv_all, preferred_element_type=jnp.float32
        ).astype(jnp.bfloat16),
        "gx",
    ).astype(jnp.float32)
    hidden_part, gain_zero = norm_one_back(normed_one_grad)
    input_full = resid_grad + hidden_part
    input_grad = lax.dynamic_slice_in_dim(input_full, gx_index * feat_share, feat_share, 1)
    gains_grad = jnp.stack([gain_zero, gain_one, gain_two, gain_three], axis=0)
    grad_qkv, grad_out, grad_gains = (
        lax.psum_scatter(
            qkv_weight_grad.astype(jnp.bfloat16), "gy", scatter_dimension=0, tiled=True
        ).astype(jnp.float32),
        lax.psum_scatter(
            out_weight_grad.astype(jnp.bfloat16), "gy", scatter_dimension=1, tiled=True
        ).astype(jnp.float32),
        lax.psum_scatter(
            gains_grad.astype(jnp.bfloat16), "gy", scatter_dimension=1, tiled=True
        ).astype(jnp.float32),
    )
    moment_qkv_new, square_qkv_new, update_qkv = adamw_step(
        qkv_weight, grad_qkv, moment_qkv, square_qkv
    )
    moment_out_new, square_out_new, update_out = adamw_step(
        out_weight, grad_out, moment_out, square_out
    )
    moment_gate_up_new, square_gate_up_new, update_gate_up = adamw_step(
        gate_up_weight, grad_gate_up, moment_gate_up, square_gate_up
    )
    moment_down_new, square_down_new, update_down = adamw_step(
        down_weight, grad_down, moment_down, square_down
    )
    moment_gains_new, square_gains_new, update_gains = adamw_step(
        norm_gains, grad_gains, moment_gains, square_gains
    )
    return (
        block_out,
        input_grad,
        grad_qkv,
        grad_out,
        grad_gate_up,
        grad_down,
        grad_gains,
        moment_qkv_new,
        moment_out_new,
        moment_gate_up_new,
        moment_down_new,
        moment_gains_new,
        square_qkv_new,
        square_out_new,
        square_gate_up_new,
        square_down_new,
        square_gains_new,
        update_qkv,
        update_out,
        update_gate_up,
        update_down,
        update_gains,
    )


def solution(mesh):
    return jax.shard_map(
        local,
        mesh=mesh,
        in_specs=(
            P("gy", "gx"),
            P("gy", "gx"),
            P(),
            P("gy", "gx", None),
            P("gx", "gy"),
            P("gy", None, "gx"),
            P("gx", "gy"),
            P(None, "gy"),
            P("gy", "gx", None),
            P("gx", "gy"),
            P("gy", None, "gx"),
            P("gx", "gy"),
            P(None, "gy"),
            P("gy", "gx", None),
            P("gx", "gy"),
            P("gy", None, "gx"),
            P("gx", "gy"),
            P(None, "gy"),
        ),
        out_specs=(
            P("gy", "gx"),
            P("gy", "gx"),
            P("gy", "gx", None),
            P("gx", "gy"),
            P("gy", None, "gx"),
            P("gx", "gy"),
            P(None, "gy"),
            P("gy", "gx", None),
            P("gx", "gy"),
            P("gy", None, "gx"),
            P("gx", "gy"),
            P(None, "gy"),
            P("gy", "gx", None),
            P("gx", "gy"),
            P("gy", None, "gx"),
            P("gx", "gy"),
            P(None, "gy"),
            P("gy", "gx", None),
            P("gx", "gy"),
            P("gy", None, "gx"),
            P("gx", "gy"),
            P(None, "gy"),
        ),
        check_vma=False,
    )
```

profile of v0, /device:TPU:0, one launch (start us, length us, event | category | flops | bytes accessed | tf_op | source)
XLA Modules:
  0.0 2062.9 jit_solution(44479979888443861)
XLA Ops:
  9.5 32.5 %all-gather = bf16[8,288,4]{1,2,0:T(4,128)(2,1)S(1)} all-gather(bf16[1,288,4]{1,2,0:T(4,128)(2,1)} %bitcast.192), channel_id=1, replica_groups=mesh['gx'=4,'gy'=8] {'gy'}, dimensions={0}, use_global_device_ids=true | all-gather | bytes 20736 | tf_op jit(solution)/shard_map/all_gather | solution.py:107
  55.8 58.8 %all-gather.10.cloned.1.call-done = bf16[2304,1,1024]{2,0,1:T(8,128)(2,1)} async-done(((bf16[288,1,1024]{2,0,1:T(8,128)(2,1)}), bf16[2304,1,1024]{2,0,1:T(8,128)(2,1)}) %all-gather.10.cloned.1.call-update) | async-done | bytes 4718608 | tf_op jit(solution)/shard_map/all_gather | solution.py:105
  114.6 4.4 fusion.51
  126.9 4.1 collective-permute-start.2
  136.1 13.1 collective-permute-start.5
  154.7 15.8 collective-permute-done.3
  171.6 15.6 collective-permute-done.4
  188.2 6.3 collective-permute-done.5
  204.0 4.6 fusion.137
  213.7 97.8 %all-reduce.5.cloned.1.call-done = f32[384,2304]{1,0:T(8,128)} async-done(((f32[384,2304]{1,0:T(8,128)}), f32[384,2304]{1,0:T(8,128)}) %all-reduce.5.cloned.1.call-update) | async-done | bytes 3538960 | tf_op jit(solution)/shard_map/psum | solution.py:174
  314.6 4.0 multiply_reduce_fusion.6
  319.8 400.5 %all-gather.14.cloned.1.call-done = bf16[2304,2,2304]{2,0,1:T(8,128)(2,1)} async-done(((bf16[288,2,2304]{2,0,1:T(8,128)(2,1)}), bf16[2304,2,2304]{2,0,1:T(8,128)(2,1)}) %all-gather.14.cloned.1.call-update) | async-done | bytes 21233680 | tf_op jit(solution)/shard_map/all_gather | solution.py:110
  720.3 13.5 fusion.100
  739.2 135.3 %all-gather.16.cloned.1.call-done = bf16[2304,2304]{0,1:T(8,128)(2,1)} async-done(((bf16[2304,288]{0,1:T(8,128)(2,1)}), bf16[2304,2304]{0,1:T(8,128)(2,1)}) %all-gather.16.cloned.1.call-update) | async-done | bytes 10616848 | tf_op jit(solution)/shard_map/all_gather | solution.py:111
  874.5 10.7 fusion.138
  885.7 9.3 all-gather.18.cloned.1.call-done
  895.0 3.8 copy.156
  898.8 74.0 %all-reduce.7.cloned.1.call-done = f32[384,2304]{1,0:T(8,128)} async-done(((f32[384,2304]{1,0:T(8,128)}), f32[384,2304]{1,0:T(8,128)}) %all-reduce.7.cloned.1.call-update) | async-done | bytes 3538960 | tf_op jit(solution)/shard_map/psum | solution.py:184
  976.9 3.8 fusion.43
  982.9 9.0 fusion.50
  991.9 15.8 convolution_bitcast_fusion
  1009.2 73.6 %all-reduce.9.cloned.1.call-done = f32[384,2304]{1,0:T(8,128)} async-done(((f32[384,2304]{1,0:T(8,128)}), f32[384,2304]{1,0:T(8,128)}) %all-reduce.9.cloned.1.call-update) | async-done | bytes 3538960 | tf_op jit(solution)/shard_map/psum | solution.py:218
  1082.8 4.7 multiply_reduce_fusion
  1087.6 4.5 multiply_reduce_fusion.1
  1096.9 6.1 fusion.1
  1103.0 5.3 fusion.31
  1108.3 7.0 fusion
  1124.9 25.7 %collective-permute-done.10 = bf16[384,1,512]{2,0,1:T(8,128)(2,1)S(1)} collective-permute-done((bf16[384,1,512]{2,0,1:T(8,128)(2,1)S(1)}, bf16[384,1,512]{2,0,1:T(8,128)(2,1)S(1)}, u32[]{:S(2)}, u32[]{:S(2)}) %collective-permute-start.10) | collective-permute-done | bytes 393248 | tf_op jit(solution)/shard_map/ppermute | solution.py:29
  1155.1 3.8 collective-permute-done.7
  1161.0 31.6 %collective-permute-done.9 = bf16[384,1,512]{2,0,1:T(8,128)(2,1)} collective-permute-done((bf16[384,1,512]{2,0,1:T(8,128)(2,1)}, bf16[384,1,512]{2,0,1:T(8,128)(2,1)}, u32[]{:S(2)}, u32[]{:S(2)}) %collective-permute-start.9) | collective-permute-done | bytes 393248 | tf_op jit(solution)/shard_map/ppermute | solution.py:29
  1195.9 5.7 fusion.15
  1203.6 41.0 %all-reduce.11.cloned.1.call-done = bf16[384,2304]{1,0:T(8,128)(2,1)} async-done(((bf16[384,2304]{1,0:T(8,128)(2,1)}), bf16[384,2304]{1,0:T(8,128)(2,1)}) %all-reduce.11.cloned.1.call-update) | async-done | bytes 1769488 | tf_op jit(solution)/shard_map/psum | solution.py:274
  1244.6 5.1 fusion.35
  1252.3 3.8 convolution_convert_fusion.3
  1256.2 5.8 fusion.8
  1263.5 9.5 convolution_convert_fusion.1
  1273.7 18.4 convolution_convert_fusion
  1302.4 12.7 reduce-scatter.16.cloned.1.call-done
  1316.7 71.1 %reduce-scatter.10.cloned.1.call-done = bf16[512,288]{0,1:T(8,128)(2,1)} async-done(((bf16[512,2304]{0,1:T(8,128)(2,1)}), bf16[512,288]{0,1:T(8,128)(2,1)}) %reduce-scatter.10.cloned.1.call-update) | async-done | bytes 294928 | tf_op jit(solution)/shard_map/reduce_scatter | solution.py:288
  1390.8 96.2 %reduce-scatter.8.cloned.1.call-done = bf16[288,1,1024]{2,0,1:T(8,128)(2,1)} async-done(((bf16[2304,1,1024]{2,0,1:T(8,128)(2,1)}), bf16[288,1,1024]{2,0,1:T(8,128)(2,1)}) %reduce-scatter.8.cloned.1.call-update) | async-done | bytes 589840 | tf_op jit(solution)/shard_map/reduce_scatter | solution.py:285
  1498.1 172.1 %reduce-scatter.14.cloned.1.call-done = bf16[2304,288]{0,1:T(8,128)(2,1)} async-done(((bf16[2304,2304]{0,1:T(8,128)(2,1)}), bf16[2304,288]{0,1:T(8,128)(2,1)}) %reduce-scatter.14.cloned.1.call-update) | async-done | bytes 1327120 | tf_op jit(solution)/shard_map/reduce_scatter | solution.py:214
  1670.2 7.9 add_multiply_fusion.1
  1678.0 341.6 %reduce-scatter.12.cloned.1.call-done = bf16[288,2,2304]{2,0,1:T(8,128)(2,1)} async-done(((bf16[2304,2,2304]{2,0,1:T(8,128)(2,1)}), bf16[288,2,2304]{2,0,1:T(8,128)(2,1)}) %reduce-scatter.12.cloned.1.call-update) | async-done | bytes 2654224 | tf_op jit(solution)/shard_map/reduce_scatter | solution.py:211
  2019.6 9.0 add_multiply_fusion
  2028.7 9.0 copy.182
  2037.6 6.5 copy.184
  2044.1 6.7 copy.186
  2050.8 5.1 copy.180
  (284 shorter events, 125.3 us)
Async XLA Ops:
  7.2 45.1 %all-gather.8.cloned.1.call-start = ((), (), s32[]{:S(2)}) async-start(), calls=%async_computation.5 | async-start | bytes 2211840 | tf_op jit(solution)/shard_map/all_gather | solution.py:101
  7.9 106.7 %all-gather.10.cloned.1.call-start = ((), (), s32[]{:S(2)}) async-start(), calls=%async_computation.6 | async-start | bytes 5308416 | tf_op jit(solution)/shard_map/all_gather | solution.py:105
  8.7 194.6 %all-gather.12.cloned.1.call-start = ((), (), s32[]{:S(2)}) async-start(), calls=%async_computation.7 | async-start | bytes 2654208 | tf_op jit(solution)/shard_map/all_gather | solution.py:106
  9.4 302.2 %all-reduce.5.cloned.1.call-start = ((), (), s32[]{:S(2)}) async-start(), calls=%async_computation.8 | async-start | bytes 7077888 | tf_op jit(solution)/shard_map/psum | solution.py:174
  9.5 109.5 %copy-start.70 = (f32[128]{0:T(128)}, f32[128]{0:T(128)S(1)}, u32[]{:S(2)}) copy-start(f32[128]{0:T(128)S(1)} %multiply_exponential_fusion) | copy-start | bytes 1540
  42.8 71.8 %copy-start.43 = (f32[2304]{0:T(1024)}, f32[2304]{0:T(1024)S(1)}, u32[]{:S(2)}) copy-start(f32[2304]{0:T(1024)S(1)} %get-tuple-element.121) | copy-start | bytes 27652
  49.0 87.0 %copy-start.19 = (f32[384,128]{1,0:T(8,128)}, f32[384,128]{1,0:T(8,128)S(1)}, u32[]{:S(2)}) copy-start(f32[384,128]{1,0:T(8,128)S(1)} %get-tuple-element.171) | copy-start | bytes 589828
  52.3 147.1 %copy-start.13 = (pred[384,2688]{0,1:T(8,128)(4,1)}, pred[384,2688]{0,1:T(8,128)(4,1)S(1)}, u32[]{:S(2)}) copy-start(pred[384,2688]{0,1:T(8,128)(4,1)S(1)} %compare_and_fusion) | copy-start | bytes 3096580
  55.3 63.7 %copy-start.1 = (bf16[384,2304]{1,0:T(8,128)(2,1)}, bf16[384,2304]{1,0:T(8,128)(2,1)S(1)}, u32[]{:S(2)}) copy-start(bf16[384,2304]{1,0:T(8,128)(2,1)S(1)} %copy.149) | copy-start | bytes 5308420
  55.8 63.2 %copy-start.61 = (f32[384]{0:T(512)}, f32[384]{0:T(512)S(1)}, u32[]{:S(2)}) copy-start(f32[384]{0:T(512)S(1)} %multiply_reduce_fusion.8) | copy-start | bytes 4612
  55.8 63.2 %copy-start.53 = (f32[384]{0:T(512)}, f32[384]{0:T(512)S(1)}, u32[]{:S(2)}) copy-start(f32[384]{0:T(512)S(1)} %fusion.109) | copy-start | bytes 4612
  120.8 15.3 collective-permute-start
  124.0 26.2 %collective-permute-start.1 = (bf16[384,1,512]{2,0,1:T(8,128)(2,1)}, bf16[384,1,512]{2,0,1:T(8,128)(2,1)}, u32[]{:S(2)}, u32[]{:S(2)}) collective-permute-start(bf16[384,1,512]{2,0,1:T(8,128)(2,1)} %get-tuple-element.165), channel_id=1, source_target_pairs={{0,2},{1,3},{2,4},{3,5},{4,6},{5,7},{8,10},{9,11},{10,12},{11,13},... | collective-permute-start | bytes 1179656 | tf_op jit(solution)/shard_map/ppermute | solution.py:29
  126.9 26.8 %collective-permute-start.2 = (bf16[384,1,512]{2,0,1:T(8,128)(2,1)}, bf16[384,1,512]{2,0,1:T(8,128)(2,1)}, u32[]{:S(2)}, u32[]{:S(2)}) collective-permute-start(bf16[384,1,512]{2,0,1:T(8,128)(2,1)} %get-tuple-element.165), channel_id=1, source_target_pairs={{0,3},{1,4},{2,5},{3,6},{4,7},{8,11},{9,12},{10,13},{11,14},{12,15... | collective-permute-start | bytes 1179656 | tf_op jit(solution)/shard_map/ppermute | solution.py:29
  131.0 39.5 %collective-permute-start.3 = (bf16[384,1,512]{2,0,1:T(8,128)(2,1)}, bf16[384,1,512]{2,0,1:T(8,128)(2,1)}, u32[]{:S(2)}, u32[]{:S(2)}) collective-permute-start(bf16[384,1,512]{2,0,1:T(8,128)(2,1)} %get-tuple-element.165), channel_id=1, source_target_pairs={{0,4},{1,5},{2,6},{3,7},{8,12},{9,13},{10,14},{11,15},{16,20},{17,... | collective-permute-start | bytes 1179656 | tf_op jit(solution)/shard_map/ppermute | solution.py:29
  133.0 54.1 %collective-permute-start.4 = (bf16[384,1,512]{2,0,1:T(8,128)(2,1)}, bf16[384,1,512]{2,0,1:T(8,128)(2,1)}, u32[]{:S(2)}, u32[]{:S(2)}) collective-permute-start(bf16[384,1,512]{2,0,1:T(8,128)(2,1)} %get-tuple-element.165), channel_id=1, source_target_pairs={{0,5},{1,6},{2,7},{8,13},{9,14},{10,15},{16,21},{17,22},{18,23},{2... | collective-permute-start | bytes 1179656 | tf_op jit(solution)/shard_map/ppermute | solution.py:29
  136.1 60.8 %copy-start.25 = (f32[384,2,128]{2,0,1:T(8,128)}, f32[384,2,128]{2,0,1:T(8,128)S(1)}, u32[]{:S(2)}) copy-start(f32[384,2,128]{2,0,1:T(8,128)S(1)} %get-tuple-element.159) | copy-start | bytes 1179652
  136.1 60.8 %copy-start.27 = (f32[384,2,128]{2,0,1:T(8,128)}, f32[384,2,128]{2,0,1:T(8,128)S(1)}, u32[]{:S(2)}) copy-start(f32[384,2,128]{2,0,1:T(8,128)S(1)} %get-tuple-element.160) | copy-start | bytes 1179652
  136.1 58.4 %collective-permute-start.5 = (bf16[384,1,512]{2,0,1:T(8,128)(2,1)}, bf16[384,1,512]{2,0,1:T(8,128)(2,1)S(1)}, u32[]{:S(2)}, u32[]{:S(2)}) collective-permute-start(bf16[384,1,512]{2,0,1:T(8,128)(2,1)} %get-tuple-element.165), channel_id=1, source_target_pairs={{0,6},{1,7},{8,14},{9,15},{16,22},{17,23},{24,30},{25,31}} | collective-permute-start | bytes 1179656 | tf_op jit(solution)/shard_map/ppermute | solution.py:29
  208.6 511.7 %all-gather.14.cloned.1.call-start = ((), (), s32[]{:S(2)}) async-start(), calls=%async_computation.9 | async-start | bytes 23887872 | tf_op jit(solution)/shard_map/all_gather | solution.py:110
  212.1 662.3 %all-gather.16.cloned.1.call-start = ((), (), s32[]{:S(2)}) async-start(), calls=%async_computation.10 | async-start | bytes 11943936 | tf_op jit(solution)/shard_map/all_gather | solution.py:111
  212.7 682.3 %all-gather.18.cloned.1.call-start = ((), (), s32[]{:S(2)}) async-start(), calls=%async_computation.12 | async-start | bytes 2211840 | tf_op jit(solution)/shard_map/all_gather | solution.py:102
  213.4 759.4 %all-reduce.7.cloned.1.call-start = ((), (), s32[]{:S(2)}) async-start(), calls=%async_computation.11 | async-start | bytes 7077888 | tf_op jit(solution)/shard_map/psum | solution.py:184
  885.1 197.6 %all-reduce.9.cloned.1.call-start = ((), (), s32[]{:S(2)}) async-start(), calls=%async_computation.13 | async-start | bytes 7077888 | tf_op jit(solution)/shard_map/psum | solution.py:218
  1007.7 236.9 %all-reduce.11.cloned.1.call-start = ((), (), s32[]{:S(2)}) async-start(), calls=%async_computation.14 | async-start | bytes 3538944 | tf_op jit(solution)/shard_map/psum | solution.py:274
  1116.9 35.2 %copy-start.42 = (bf16[2688,1,512]{2,0,1:T(8,128)(2,1)S(1)}, bf16[2688,1,512]{2,0,1:T(8,128)(2,1)}, u32[]{:S(2)}) copy-start(bf16[2688,1,512]{2,0,1:T(8,128)(2,1)} %copy-done.41) | copy-start | bytes 8257540
  1118.2 32.3 %collective-permute-start.10 = (bf16[384,1,512]{2,0,1:T(8,128)(2,1)S(1)}, bf16[384,1,512]{2,0,1:T(8,128)(2,1)S(1)}, u32[]{:S(2)}, u32[]{:S(2)}) collective-permute-start(bf16[384,1,512]{2,0,1:T(8,128)(2,1)S(1)} %get-tuple-element.150), channel_id=1, source_target_pairs={{5,0},{6,1},{7,2},{13,8},{14,9},{15,10},{21,16},{22,17},{23,18},{2... | collective-permute-start | bytes 1179656 | tf_op jit(solution)/shard_map/ppermute | solution.py:29
  1119.7 35.5 %collective-permute-start.11 = (bf16[384,1,512]{2,0,1:T(8,128)(2,1)}, bf16[384,1,512]{2,0,1:T(8,128)(2,1)}, u32[]{:S(2)}, u32[]{:S(2)}) collective-permute-start(bf16[384,1,512]{2,0,1:T(8,128)(2,1)} %get-tuple-element.149), channel_id=1, source_target_pairs={{6,0},{7,1},{14,8},{15,9},{22,16},{23,17},{30,24},{31,25}} | collective-permute-start | bytes 1179656 | tf_op jit(solution)/shard_map/ppermute | solution.py:29
  1121.0 34.2 %collective-permute-start.6 = (bf16[384,1,512]{2,0,1:T(8,128)(2,1)}, bf16[384,1,512]{2,0,1:T(8,128)(2,1)}, u32[]{:S(2)}, u32[]{:S(2)}) collective-permute-start(bf16[384,1,512]{2,0,1:T(8,128)(2,1)} %get-tuple-element.148), channel_id=1, source_target_pairs={{1,0},{2,1},{3,2},{4,3},{5,4},{6,5},{7,6},{9,8},{10,9},{11,10},{12... | collective-permute-start | bytes 1179656 | tf_op jit(solution)/shard_map/ppermute | solution.py:29
  1122.3 36.6 %collective-permute-start.7 = (bf16[384,1,512]{2,0,1:T(8,128)(2,1)}, bf16[384,1,512]{2,0,1:T(8,128)(2,1)}, u32[]{:S(2)}, u32[]{:S(2)}) collective-permute-start(bf16[384,1,512]{2,0,1:T(8,128)(2,1)} %get-tuple-element.153), channel_id=1, source_target_pairs={{2,0},{3,1},{4,2},{5,3},{6,4},{7,5},{10,8},{11,9},{12,10},{13,11},... | collective-permute-start | bytes 1179656 | tf_op jit(solution)/shard_map/ppermute | solution.py:29
  1123.6 37.5 %collective-permute-start.8 = (bf16[384,1,512]{2,0,1:T(8,128)(2,1)}, bf16[384,1,512]{2,0,1:T(8,128)(2,1)}, u32[]{:S(2)}, u32[]{:S(2)}) collective-permute-start(bf16[384,1,512]{2,0,1:T(8,128)(2,1)} %get-tuple-element.152), channel_id=1, source_target_pairs={{3,0},{4,1},{5,2},{6,3},{7,4},{11,8},{12,9},{13,10},{14,11},{15,12... | collective-permute-start | bytes 1179656 | tf_op jit(solution)/shard_map/ppermute | solution.py:29
  1150.5 42.1 %collective-permute-start.9 = (bf16[384,1,512]{2,0,1:T(8,128)(2,1)}, bf16[384,1,512]{2,0,1:T(8,128)(2,1)}, u32[]{:S(2)}, u32[]{:S(2)}) collective-permute-start(bf16[384,1,512]{2,0,1:T(8,128)(2,1)} %get-tuple-element.151), channel_id=1, source_target_pairs={{4,0},{5,1},{6,2},{7,3},{12,8},{13,9},{14,10},{15,11},{20,16},{21,... | collective-permute-start | bytes 1179656 | tf_op jit(solution)/shard_map/ppermute | solution.py:29
  1155.1 39.5 %copy-start.71 = (f32[128]{0:T(128)S(1)}, f32[128]{0:T(128)}, u32[]{:S(2)}) copy-start(f32[128]{0:T(128)} %copy-done.70) | copy-start | bytes 1540
  1155.1 40.8 %copy-start.33 = (bf16[384,1,2,256]{0,3,2,1:T(8,128)(2,1)S(1)}, bf16[384,1,2,256]{0,3,2,1:T(8,128)(2,1)}, u32[]{:S(2)}) copy-start(bf16[384,1,2,256]{0,3,2,1:T(8,128)(2,1)} %copy.161) | copy-start | bytes 1179652
  1195.9 48.7 %copy-start.2 = (bf16[384,2304]{1,0:T(8,128)(2,1)S(1)}, bf16[384,2304]{1,0:T(8,128)(2,1)}, u32[]{:S(2)}) copy-start(bf16[384,2304]{1,0:T(8,128)(2,1)} %copy-done.1) | copy-start | bytes 5308420
  1195.9 48.7 %copy-start.44 = (f32[2304]{0:T(1024)S(1)}, f32[2304]{0:T(1024)}, u32[]{:S(2)}) copy-start(f32[2304]{0:T(1024)} %copy-done.43) | copy-start | bytes 27652
  1195.9 48.7 %copy-start.54 = (f32[384]{0:T(512)S(1)}, f32[384]{0:T(512)}, u32[]{:S(2)}) copy-start(f32[384]{0:T(512)} %copy-done.53) | copy-start | bytes 4612
  1201.7 113.4 %reduce-scatter.16.cloned.1.call-start = ((), (), s32[]{:S(2)}) async-start(), calls=%async_computation.19 | async-start | bytes 663552
  1203.6 48.7 %copy-start.24 = (bf16[384,2304]{1,0:T(8,128)(2,1)S(1)}, bf16[384,2304]{1,0:T(8,128)(2,1)}, u32[]{:S(2)}) copy-start(bf16[384,2304]{1,0:T(8,128)(2,1)} %copy-done.23) | copy-start | bytes 5308420
  1252.2 135.6 %reduce-scatter.10.cloned.1.call-start = ((), (), s32[]{:S(2)}) async-start(), calls=%async_computation.16 | async-start | bytes 2654208 | tf_op jit(solution)/shard_map/reduce_scatter | solution.py:288
  1256.1 230.8 %reduce-scatter.8.cloned.1.call-start = ((), (), s32[]{:S(2)}) async-start(), calls=%async_computation.15 | async-start | bytes 5308416 | tf_op jit(solution)/shard_map/reduce_scatter | solution.py:285
  1262.0 408.1 %reduce-scatter.14.cloned.1.call-start = ((), (), s32[]{:S(2)}) async-start(), calls=%async_computation.18 | async-start | bytes 11943936 | tf_op jit(solution)/shard_map/reduce_scatter | solution.py:214
  1273.0 746.6 %reduce-scatter.12.cloned.1.call-start = ((), (), s32[]{:S(2)}) async-start(), calls=%async_computation.17 | async-start | bytes 23887872 | tf_op jit(solution)/shard_map/reduce_scatter | solution.py:211
  1297.2 18.9 copy-start.65
  1297.2 90.7 %copy-start.29 = (bf16[512,288]{0,1:T(8,128)(2,1)S(1)}, bf16[512,288]{0,1:T(8,128)(2,1)}, u32[]{:S(2)}) copy-start(bf16[512,288]{0,1:T(8,128)(2,1)} %param.22) | copy-start | bytes 884740
  1301.2 185.8 %copy-start.17 = (bf16[288,1,1024]{2,0,1:T(8,128)(2,1)S(1)}, bf16[288,1,1024]{2,0,1:T(8,128)(2,1)}, u32[]{:S(2)}) copy-start(bf16[288,1,1024]{2,0,1:T(8,128)(2,1)} %param.21) | copy-start | bytes 1769476
  1301.2 185.8 %copy-start.30 = (f32[288,1,1024]{2,1,0:T(1,128)S(1)}, f32[288,1,1024]{2,1,0:T(1,128)}, u32[]{:S(2)}) copy-start(f32[288,1,1024]{2,1,0:T(1,128)} %param.31) | copy-start | bytes 3538948
  1498.1 521.5 %copy-start.11 = (bf16[288,2,2304]{2,1,0:T(2,128)(2,1)S(1)}, bf16[288,2,2304]{2,1,0:T(2,128)(2,1)}, u32[]{:S(2)}) copy-start(bf16[288,2,2304]{2,1,0:T(2,128)(2,1)} %param.23) | copy-start | bytes 7962628
  (52 other events, 259.5 us)
Sparse Core Ops, SparseCore 0:
  9.6 23.4 all-gather.7
  35.2 79.3 all-gather.9
  116.8 70.2 all-gather.11
  208.7 102.7 all-reduce.4
  313.5 406.7 all-gather.13
  722.3 152.0 all-gather.15
  876.0 18.9 all-gather.17
  897.9 74.8 all-reduce.6
  1007.8 74.9 all-reduce.8
  1201.8 42.7 all-reduce.10
  1252.3 62.7 reduce-scatter.15
  1319.0 68.7 reduce-scatter.9
  1392.1 94.8 reduce-scatter.7
  1490.4 179.7 reduce-scatter.13
  1673.9 345.6 reduce-scatter.11
where the time goes:
time: 2070 us; the launch traced here: 2060 us
  waiting for transfers between devices  1690 us (82%)
  matrix products  122 us (6%)
  other arithmetic  83.5 us (4%)
  local copies, waits for them, and re-layouts  81 us (4%)
  starting transfers between devices  37.5 us (2%)
  blocking collectives  32.5 us (2%)
    all_gather x1, waiting for transfers between devices, local(): lax.all_gather(gate_up_weight, 'gy', axis=0, tiled=True)  400 us
    reduce_scatter x1, waiting for transfers between devices, local(): lax.psum_scatter(gate_up_weight_grad.astype(jnp.bfloat16), 'gy', scatter_...  342 us
    reduce_scatter x1, waiting for transfers between devices, local(): lax.psum_scatter(down_weight_grad.astype(jnp.bfloat16), 'gy', scatter_dim...  172 us
    all_gather x1, waiting for transfers between devices, local(): lax.all_gather(down_weight, 'gy', axis=1, tiled=True)  135 us
    ppermute x12, waiting for transfers between devices, shifted(): return lax.ppermute(block, axis, route)  103 us
    psum x1, waiting for transfers between devices, local(): lax.psum(jnp.dot(attn_low, out_all, preferred_element_type=jnp.float32),...  97.8 us
    reduce_scatter x1, waiting for transfers between devices, local(): lax.psum_scatter(qkv_weight_grad.astype(jnp.bfloat16), 'gy', scatter_dime...  96.2 us
    psum x1, waiting for transfers between devices, local(): lax.psum(jnp.dot(hidden_act, down_all, preferred_element_type=jnp.float32...  74 us
  transfers between devices with their start and end apart: 27, of which 21 were waited for; matrix products, arithmetic and copies ran while one was open for 7% of the time, Pallas kernels for 0%

commit v1 on v0

v1 whole, which is shorter than its diff:
```python
import math

import jax
import jax.numpy as jnp
from jax import lax
from jax.sharding import Mesh, PartitionSpec as P

HEADS = 8
KV = 4
HEAD = 256
MEAN_LEN = 1024


NORM_EPS = 1e-06
SOFT_CAP = 50.0
MASKED_SCORE = -1e30
BETA_ONE = 0.9
BETA_TWO = 0.95
FIRST_FIX = 1.0 - 0.9**10
SECOND_FIX = 1.0 - 0.95**10
LEARN_RATE = 0.05
WEIGHT_DECAY = 0.1
ADAM_EPS = 1e-08


def shifted(block, axis, distance):
    devices = range(lax.axis_size(axis))
    route = [(i - distance, i) for i in devices if i - distance in devices]
    return lax.ppermute(block, axis, route)


def rms_norm(values, gain_row):
    return (
        values
        * lax.rsqrt(jnp.mean(values * values, axis=-1, keepdims=True) + NORM_EPS)
        * (1.0 + gain_row)
    )


def rotate(tensor, cosine, sine_part):
    half_dim = tensor.shape[-1] // 2
    leading = tensor[..., :half_dim]
    trailing = tensor[..., half_dim:]
    return jnp.concatenate(
        [leading * cosine - trailing * sine_part, trailing * cosine + leading * sine_part], axis=-1
    )


def geglu_mix(gate_pre, up_pre):
    return jax.nn.gelu(gate_pre, approximate=True) * up_pre


def adamw_step(weight, gradient, moment, square):
    weight_wide = weight.astype(jnp.float32)
    moment_new = BETA_ONE * moment + (1.0 - BETA_ONE) * gradient
    square_new = BETA_TWO * square + (1.0 - BETA_TWO) * gradient * gradient
    update = -LEARN_RATE * (
        moment_new / FIRST_FIX / (jnp.sqrt(square_new / SECOND_FIX) + ADAM_EPS)
        + WEIGHT_DECAY * weight_wide
    )
    return (moment_new, square_new, update)


def capped_scores(query_rot, key_part, allowed):
    raw_scores = jnp.einsum(
        "qkgd,skd->kgqs", query_rot, key_part, preferred_element_type=jnp.float32
    )
    bent_raw = jnp.tanh(raw_scores / SOFT_CAP)
    return (bent_raw, jnp.where(allowed, SOFT_CAP * bent_raw, MASKED_SCORE))


def split_axes(mesh):
    gx_count, gy_count = mesh.shape["gx"], mesh.shape["gy"]
    fold = 4
    return Mesh(mesh.devices.reshape(gx_count, fold, gy_count // fold), ("gx", "gf", "gt"))


def exchange(blocks, axis):
    count = lax.axis_size(axis)
    mine = lax.axis_index(axis)
    received = blocks
    for step in range(1, count):
        target = (mine + step) % count
        sent = lax.dynamic_index_in_dim(blocks, target, 0, keepdims=True)
        got = lax.ppermute(sent, axis, [(i, (i + step) % count) for i in range(count)])
        received = lax.dynamic_update_slice_in_dim(received, got, (mine - step) % count, 0)
    return received


def collect(block, axis):
    if lax.axis_size(axis) != 2:
        return lax.all_gather(block, axis, axis=1)
    other = lax.ppermute(block, axis, [(0, 1), (1, 0)])
    first = lax.axis_index(axis) == 0
    return jnp.stack([jnp.where(first, block, other), jnp.where(first, other, block)], axis=1)


def reduce_out(blocks, axis):
    if lax.axis_size(axis) != 2:
        return lax.psum_scatter(blocks, axis, scatter_dimension=1, tiled=False)
    mine = lax.axis_index(axis)
    sent = lax.dynamic_index_in_dim(blocks, 1 - mine, 1, keepdims=False)
    kept = lax.dynamic_index_in_dim(blocks, mine, 1, keepdims=False)
    got = lax.ppermute(sent, axis, [(0, 1), (1, 0)])
    return (kept.astype(jnp.float32) + got.astype(jnp.float32)).astype(jnp.bfloat16)


def local(
    hidden_in,
    out_grad,
    seq_ids,
    qkv_weight,
    out_weight,
    gate_up_weight,
    down_weight,
    norm_gains,
    moment_qkv,
    moment_out,
    moment_gate_up,
    moment_down,
    moment_gains,
    square_qkv,
    square_out,
    square_gate_up,
    square_down,
    square_gains,
):
    f32, bf16 = jnp.float32, jnp.bfloat16
    rows_here = hidden_in.shape[0]
    local_kv = qkv_weight.shape[1]
    group_size = HEADS // KV
    gx_count = lax.axis_size("gx")
    fold = lax.axis_size("gf")
    spread = lax.axis_size("gt")
    gy_count = fold * spread
    gy_index = lax.axis_index("gf") * spread + lax.axis_index("gt")
    gx_index = lax.axis_index("gx")
    gy = ("gf", "gt")
    team = ("gx", "gf")
    part = rows_here // gx_count
    feat = hidden_in.shape[1] * gx_count
    depth = gate_up_weight.shape[0]
    ff_here = gate_up_weight.shape[2]
    ff_part = ff_here // fold
    reach_back = min((2 * MEAN_LEN - 2) // rows_here + 1, gy_count - 1)
    whole_keys = gy_count == reach_back + 2 or gy_count == reach_back + 1

    hidden_all = lax.all_gather(hidden_in, "gx", axis=1, tiled=True)
    qkv_all = lax.all_gather(qkv_weight[:, 0], gy, axis=0, tiled=True)
    gains_all = lax.all_gather(norm_gains, gy, axis=1, tiled=True)
    out_all = lax.all_gather(out_weight, gy, axis=1, tiled=True)

    three = jnp.stack([gate_up_weight[:, 0], gate_up_weight[:, 1], down_weight.T], axis=0)
    three = three.reshape(3, depth, fold, ff_part).transpose(2, 0, 1, 3)
    gate_up_got = exchange(three[:, :2], "gf")
    down_got = exchange(three[:, 2], "gf")
    gate_w = collect(gate_up_got[:, 0], "gt").reshape(feat, ff_part)
    up_w = collect(gate_up_got[:, 1], "gt").reshape(feat, ff_part)
    down_w = collect(down_got, "gt").reshape(feat, ff_part)

    gains_wide = gains_all.astype(f32)
    hidden_wide = hidden_all.astype(f32)
    first_row = gy_index * rows_here
    query_index = first_row + jnp.arange(rows_here, dtype=jnp.int32)
    inverse = jnp.exp(jnp.arange(HEAD // 2, dtype=f32) * (-2.0 * math.log(10000.0) / HEAD))
    angles = query_index.astype(f32)[:, None] * inverse[None, :]
    cosine = jnp.cos(angles)
    sine_part = jnp.sin(angles)
    cos_query = cosine[:, None, :]
    sin_query = sine_part[:, None, :]
    query_scale = HEAD ** (-0.5)
    normed_one = rms_norm(hidden_wide, gains_wide[0]).astype(bf16)
    projected = jnp.dot(normed_one, qkv_all, preferred_element_type=f32)
    query_raw = projected[:, : group_size * HEAD].reshape(rows_here, group_size, HEAD)
    key_raw = projected[:, group_size * HEAD : (group_size + 1) * HEAD]
    value_raw = projected[:, (group_size + 1) * HEAD :]
    query_rot = (rotate(query_raw, cos_query, sin_query) * query_scale).astype(bf16)
    key_rot = rotate(key_raw, cosine, sine_part).astype(bf16)
    key_value = jnp.concatenate([key_rot, value_raw.astype(bf16)], axis=-1)
    if whole_keys:
        key_value_all = lax.all_gather(key_value, gy, axis=0, tiled=True)
        key_index = jnp.arange(gy_count * rows_here, dtype=jnp.int32)
        key_seq = seq_ids
    else:
        kv_blocks = [key_value]
        for offset in range(1, reach_back + 1):
            kv_blocks.append(shifted(key_value, gy, offset))
        key_value_all = jnp.concatenate(kv_blocks, axis=0)
        key_index = jnp.concatenate(
            [
                (gy_index - offset) * rows_here + jnp.arange(rows_here, dtype=jnp.int32)
                for offset in range(reach_back + 1)
            ]
        )
        key_seq = jnp.concatenate(
            [
                lax.dynamic_slice_in_dim(
                    seq_ids, jnp.maximum((gy_index - offset) * rows_here, 0), rows_here, 0
                )
                for offset in range(reach_back + 1)
            ]
        )
    query_seq = lax.dynamic_slice_in_dim(seq_ids, first_row, rows_here, 0)
    allowed = (
        (key_index[None, :] >= 0)
        & (key_index[None, :] <= query_index[:, None])
        & (key_seq[None, :] == query_seq[:, None])
    )
    key_part = key_value_all[:, :HEAD]
    value_part = key_value_all[:, HEAD:]
    raw_scores = jnp.einsum("qgd,sd->gqs", query_rot, key_part, preferred_element_type=f32)
    bent_raw = jnp.tanh(raw_scores / SOFT_CAP)
    scores = jnp.where(allowed, SOFT_CAP * bent_raw, MASKED_SCORE)
    row_top = jnp.max(scores, axis=-1, keepdims=True)
    exp_scores = jnp.exp(scores - row_top)
    row_total = jnp.sum(exp_scores, axis=-1, keepdims=True)
    attn_probs = exp_scores / row_total
    probs_low = attn_probs.astype(bf16)
    attended = jnp.einsum("gqs,sd->qgd", probs_low, value_part, preferred_element_type=f32)
    attn_low = attended.astype(bf16).reshape(rows_here, group_size * HEAD)
    mixed_part = jnp.dot(attn_low, out_all, preferred_element_type=f32).astype(bf16)

    def token_sum(partial):
        shared = lax.all_to_all(partial, "gx", 0, 0, tiled=True)
        return jnp.sum(shared.reshape(gx_count, part, feat).astype(f32), axis=0)

    own = lax.dynamic_slice_in_dim(hidden_all, gx_index * part, part, 0).astype(f32)
    grad_own = lax.all_to_all(out_grad, "gx", 0, 1, tiled=True).astype(f32)
    mixed_sum = token_sum(mixed_part)
    branch_one, post_one_back = jax.vjp(rms_norm, mixed_sum, gains_wide[1])
    resid_sum = own + branch_one
    normed_two, norm_two_back = jax.vjp(rms_norm, resid_sum, gains_wide[2])
    normed_all = lax.all_gather(normed_two.astype(bf16), team, axis=0, tiled=True)
    gate_pre = jnp.dot(normed_all, gate_w, preferred_element_type=f32)
    up_pre = jnp.dot(normed_all, up_w, preferred_element_type=f32)
    hidden_act, geglu_back = jax.vjp(geglu_mix, gate_pre, up_pre)
    hidden_act = hidden_act.astype(bf16)
    down_part = jnp.einsum("tf,df->td", hidden_act, down_w, preferred_element_type=f32)
    down_sum = lax.psum_scatter(down_part.astype(bf16), team, scatter_dimension=0, tiled=True)
    down_sum = down_sum.astype(f32)
    branch_two, post_two_back = jax.vjp(rms_norm, down_sum, gains_wide[3])
    block_own = (resid_sum + branch_two).astype(bf16)
    block_out = lax.all_to_all(block_own, "gx", 1, 0, tiled=True)

    down_grad, gain_three = post_two_back(grad_own)
    down_low = lax.all_gather(down_grad.astype(bf16), team, axis=0, tiled=True)
    act_grad = jnp.dot(down_low, down_w, preferred_element_type=f32)
    gate_grad, up_grad = geglu_back(act_grad)
    gate_low, up_low = gate_grad.astype(bf16), up_grad.astype(bf16)
    normed_part = jnp.einsum("tf,df->td", gate_low, gate_w, preferred_element_type=f32)
    normed_part += jnp.einsum("tf,df->td", up_low, up_w, preferred_element_type=f32)
    normed_two_grad = lax.psum_scatter(
        normed_part.astype(bf16), team, scatter_dimension=0, tiled=True
    ).astype(f32)
    three_grad = [
        jnp.einsum("td,tf->df", left, right, preferred_element_type=f32)
        .astype(bf16)
        .reshape(fold, spread, depth, ff_part)
        for left, right in ((normed_all, gate_low), (normed_all, up_low), (down_low, hidden_act))
    ]
    gate_up_sent = jnp.stack([reduce_out(g, "gt") for g in three_grad[:2]], axis=1)
    gate_up_back = exchange(gate_up_sent, "gf").transpose(2, 1, 0, 3)
    grad_gate_up = gate_up_back.reshape(depth, 2, ff_here).astype(f32)
    down_back = exchange(reduce_out(three_grad[2], "gt"), "gf")
    grad_down = down_back.transpose(0, 2, 1).reshape(ff_here, depth).astype(f32)

    resid_part, gain_two = norm_two_back(normed_two_grad)
    resid_grad = grad_own + resid_part
    mixed_grad, gain_one = post_one_back(resid_grad)
    mixed_low = lax.all_gather(mixed_grad.astype(bf16), "gx", axis=0, tiled=True)
    attn_grad = jnp.einsum("td,cd->tc", mixed_low, out_all, preferred_element_type=f32)
    attn_grad = attn_grad.astype(bf16).reshape(rows_here, group_size, HEAD)
    out_weight_grad = jnp.einsum("tc,td->cd", attn_low, mixed_low, preferred_element_type=f32)
    prob_grad = jnp.einsum("qgd,sd->gqs", attn_grad, value_part, preferred_element_type=f32)
    row_delta = jnp.sum(attn_probs * prob_grad, axis=-1, keepdims=True)
    raw_grad = (attn_probs * (prob_grad - row_delta) * (1.0 - bent_raw * bent_raw)).astype(bf16)
    query_grad = jnp.einsum("gqs,sd->qgd", raw_grad, key_part, preferred_element_type=f32)
    key_value_grad = jnp.concatenate(
        [
            jnp.einsum("gqs,qgd->sd", raw_grad, query_rot, preferred_element_type=f32),
            jnp.einsum("gqs,qgd->sd", probs_low, attn_grad, preferred_element_type=f32),
        ],
        axis=-1,
    )
    if whole_keys:
        kv_grad_mine = lax.psum_scatter(
            key_value_grad.astype(bf16), gy, scatter_dimension=0, tiled=True
        ).astype(f32)
    else:
        kv_grad_mine = key_value_grad[:rows_here]
        for offset in range(1, reach_back + 1):
            kv_grad_mine = kv_grad_mine + shifted(
                key_value_grad[offset * rows_here : (offset + 1) * rows_here].astype(bf16),
                gy,
                -offset,
            ).astype(f32)
    key_grad = rotate(kv_grad_mine[:, :HEAD], cosine, -sine_part)
    value_grad = kv_grad_mine[:, HEAD:]
    query_raw_grad = rotate(query_grad * query_scale, cos_query, -sin_query).reshape(
        rows_here, group_size * HEAD
    )
    projected_low = jnp.concatenate([query_raw_grad, key_grad, value_grad], axis=-1).astype(bf16)
    qkv_weight_grad = jnp.einsum("td,tc->dc", normed_one, projected_low, preferred_element_type=f32)
    normed_one_part = jnp.einsum("tc,dc->td", projected_low, qkv_all, preferred_element_type=f32)
    normed_one_grad = token_sum(normed_one_part.astype(bf16))
    _, norm_one_back = jax.vjp(rms_norm, own, gains_wide[0])
    hidden_part, gain_zero = norm_one_back(normed_one_grad)
    input_grad = lax.all_to_all(resid_grad + hidden_part, "gx", 1, 0, tiled=True)
    gains_grad = jnp.stack([gain_zero, gain_one, gain_two, gain_three], axis=0)
    grad_qkv = lax.psum_scatter(
        qkv_weight_grad.astype(bf16), gy, scatter_dimension=0, tiled=True
    ).astype(f32)[:, None]
    grad_out = lax.psum_scatter(
        out_weight_grad.astype(bf16), gy, scatter_dimension=1, tiled=True
    ).astype(f32)
    gains_sum = lax.psum(gains_grad, ("gx", "gf", "gt"))
    grad_gains = lax.dynamic_slice_in_dim(gains_sum, gy_index * depth, depth, 1)

    moment_qkv_new, square_qkv_new, update_qkv = adamw_step(
        qkv_weight, grad_qkv, moment_qkv, square_qkv
    )
    moment_out_new, square_out_new, update_out = adamw_step(
        out_weight, grad_out, moment_out, square_out
    )
    moment_gate_up_new, square_gate_up_new, update_gate_up = adamw_step(
        gate_up_weight, grad_gate_up, moment_gate_up, square_gate_up
    )
    moment_down_new, square_down_new, update_down = adamw_step(
        down_weight, grad_down, moment_down, square_down
    )
    moment_gains_new, square_gains_new, update_gains = adamw_step(
        norm_gains, grad_gains, moment_gains, square_gains
    )
    return (
        block_out,
        input_grad,
        grad_qkv,
        grad_out,
        grad_gate_up,
        grad_down,
        grad_gains,
        moment_qkv_new,
        moment_out_new,
        moment_gate_up_new,
        moment_down_new,
        moment_gains_new,
        square_qkv_new,
        square_out_new,
        square_gate_up_new,
        square_down_new,
        square_gains_new,
        update_qkv,
        update_out,
        update_gate_up,
        update_down,
        update_gains,
    )


def solution(mesh):
    return jax.shard_map(
        local,
        mesh=split_axes(mesh),
        in_specs=(
            P(("gf", "gt"), "gx"),
            P(("gf", "gt"), "gx"),
            P(),
            P(("gf", "gt"), "gx", None),
            P("gx", ("gf", "gt")),
            P(("gf", "gt"), None, "gx"),
            P("gx", ("gf", "gt")),
            P(None, ("gf", "gt")),
            P(("gf", "gt"), "gx", None),
            P("gx", ("gf", "gt")),
            P(("gf", "gt"), None, "gx"),
            P("gx", ("gf", "gt")),
            P(None, ("gf", "gt")),
            P(("gf", "gt"), "gx", None),
            P("gx", ("gf", "gt")),
            P(("gf", "gt"), None, "gx"),
            P("gx", ("gf", "gt")),
            P(None, ("gf", "gt")),
        ),
        out_specs=(
            P(("gf", "gt"), "gx"),
            P(("gf", "gt"), "gx"),
            P(("gf", "gt"), "gx", None),
            P("gx", ("gf", "gt")),
            P(("gf", "gt"), None, "gx"),
            P("gx", ("gf", "gt")),
            P(None, ("gf", "gt")),
            P(("gf", "gt"), "gx", None),
            P("gx", ("gf", "gt")),
            P(("gf", "gt"), None, "gx"),
            P("gx", ("gf", "gt")),
            P(None, ("gf", "gt")),
            P(("gf", "gt"), "gx", None),
            P("gx", ("gf", "gt")),
            P(("gf", "gt"), None, "gx"),
            P("gx", ("gf", "gt")),
            P(None, ("gf", "gt")),
            P(("gf", "gt"), "gx", None),
            P("gx", ("gf", "gt")),
            P(("gf", "gt"), None, "gx"),
            P("gx", ("gf", "gt")),
            P(None, ("gf", "gt")),
        ),
        check_vma=False,
    )
```

time: 2070 us -> 1350 us (0.65)
  waiting for transfers between devices: 1690 us -> 593 us
  local copies, waits for them, and re-layouts: 81 us -> 300 us
  matrix products: 122 us -> 192 us
  blocking collectives: 32.5 us -> 97.7 us
  starting transfers between devices: 37.5 us -> 58.4 us
    reduce_scatter x4 -> x5, waiting for transfers between devices: 681 us -> 201 us  [the longest x1 97.3 us: local(): lax.psum_scatter(down_part.astype(bf16), team, scatter_dimension=0, tiled...]
    all_gather x6 -> x7, waiting for transfers between devices: 604 us -> 236 us  [the longest x1 70.4 us: local(): qkv_all = lax.all_gather(qkv_weight[:, 0], gy, axis=0, tiled=True)]
    psum x4 -> x0, waiting for transfers between devices: 286 us -> none  [the longest x1 97.8 us: local(): lax.psum(jnp.dot(attn_low, out_all, preferred_element_type=jnp.float32),...]
    dynamic_update_slice x0 -> x11, local copies, waits for them, and re-layouts: none -> 132 us  [exchange(): lax.dynamic_update_slice_in_dim(received, got, (mine - step) % count, 0)]
    dot_general x18 -> x21, matrix products: 122 us -> 182 us  [the longest x3 27 us: local(): jnp.einsum('td,tf->df', left, right, preferred_element_type=f32)]
    psum x0 -> x1, blocking collectives: none -> 54.4 us  [local(): gains_sum = lax.psum(gains_grad, ('gx', 'gf', 'gt'))]
    convert_element_type x1 -> x10, local copies, waits for them, and re-layouts: 0.09 us -> 33.3 us  [the longest x2 14.4 us: local(): grad_gate_up = gate_up_back.reshape(depth, 2, ff_here).astype(f32)]
    ppermute x12 -> x18, waiting for transfers between devices: 103 us -> 131 us  [the longest x3 56.6 us: collect(): other = lax.ppermute(block, axis, [(0, 1), (1, 0)])]
  transfers between devices with their start and end apart: 27 -> 34, of which waited for: 21 -> 18; matrix products, arithmetic and copies ran while one was open for 7% -> 32% of each run, Pallas kernels for 0% -> 0%
where the time goes in v1:
time: 1350 us; the launch traced here: 1340 us
  waiting for transfers between devices  593 us (44%)
  local copies, waits for them, and re-layouts  300 us (22%)
  matrix products  192 us (14%)
  blocking collectives  97.7 us (7%)
  other arithmetic  82.2 us (6%)
  starting transfers between devices  58.4 us (4%)
  between operations  15.6 us (1%)
    dynamic_update_slice x11, local copies, waits for them, and re-layouts, exchange(): lax.dynamic_update_slice_in_dim(received, got, (mine - step) % count, 0)  132 us
    reduce_scatter x1, waiting for transfers between devices, local(): lax.psum_scatter(down_part.astype(bf16), team, scatter_dimension=0, tiled...  97.3 us
    reduce_scatter x1, waiting for transfers between devices, local(): lax.psum_scatter(normed_part.astype(bf16), team, scatter_dimension=0, til...  88.8 us
    all_gather x1, waiting for transfers between devices, local(): qkv_all = lax.all_gather(qkv_weight[:, 0], gy, axis=0, tiled=True)  70.4 us
    all_gather x1, waiting for transfers between devices, local(): down_low = lax.all_gather(down_grad.astype(bf16), team, axis=0, tiled=True)  65.9 us
    ppermute x3, waiting for transfers between devices, collect(): other = lax.ppermute(block, axis, [(0, 1), (1, 0)])  56.6 us
    psum x1, blocking collectives, local(): gains_sum = lax.psum(gains_grad, ('gx', 'gf', 'gt'))  54.4 us
    all_gather x1, waiting for transfers between devices, local(): key_value_all = lax.all_gather(key_value, gy, axis=0, tiled=True)  52.7 us
  transfers between devices with their start and end apart: 34, of which 18 were waited for; matrix products, arithmetic and copies ran while one was open for 32% of the time, Pallas kernels for 0%

profile of v1, /device:TPU:0, one launch (start us, length us, event | category | flops | bytes accessed | tf_op | source)
XLA Modules:
  0.0 1338.1 jit_solution(14150669676064718897)
XLA Ops:
  8.7 32.5 %all-gather.1 = bf16[8,288,4]{1,2,0:T(4,128)(2,1)S(1)} all-gather(bf16[1,288,4]{1,2,0:T(4,128)(2,1)} %bitcast.254), channel_id=1, replica_groups=mesh['gx'=4,'gf'=4,'gt'=2] {'gf','gt'}, dimensions={0}, use_global_device_ids=true | all-gather | bytes 20736 | tf_op jit(solution)/shard_map/all_gather | solution.py:150
  44.1 70.4 %all-gather.22.cloned.1.call-done = bf16[2304,1,1024]{2,0,1:T(8,128)(2,1)} async-done(((bf16[288,1,1024]{2,0,1:T(8,128)(2,1)}), bf16[2304,1,1024]{2,0,1:T(8,128)(2,1)}) %all-gather.22.cloned.1.call-update) | async-done | bytes 4718608 | tf_op jit(solution)/shard_map/all_gather | solution.py:149
  127.8 52.7 %all-gather.12.cloned.1.call-done = bf16[3072,512]{1,0:T(8,128)(2,1)} async-done(((bf16[384,512]{1,0:T(8,128)(2,1)}), bf16[3072,512]{1,0:T(8,128)(2,1)}) %all-gather.12.cloned.1.call-update) | async-done | bytes 3145744 | tf_op jit(solution)/shard_map/all_gather | solution.py:181
  180.6 9.8 fusion.137
  190.3 8.9 fusion.44
  199.2 33.9 %all-gather.14.cloned.1.call-done = bf16[512,2304]{0,1:T(8,128)(2,1)} async-done(((bf16[512,288]{0,1:T(8,128)(2,1)}), bf16[512,2304]{0,1:T(8,128)(2,1)}) %all-gather.14.cloned.1.call-update) | async-done | bytes 2359312 | tf_op jit(solution)/shard_map/all_gather | solution.py:151
  243.2 20.3 %all-to-all-done = bf16[4,96,2304]{2,1,0:T(8,128)(2,1)S(1)} async-done(((bf16[4,96,2304]{2,1,0:T(8,128)(2,1)}), bf16[4,96,2304]{2,1,0:T(8,128)(2,1)S(1)}, u32[]{:S(2)}, u32[]{:S(2)}) %all-to-all-start) | async-done | bytes 1769504 | tf_op jit(solution)/shard_map/all_to_all | solution.py:224
  271.8 16.5 %slice_reduce_fusion.1 = (bf16[288,2304]{1,0:T(8,128)(2,1)}, bf16[288,2304]{1,0:T(8,128)(2,1)}) fusion(bf16[288,2,2304]{2,1,0:T(2,128)(2,1)S(1)} %copy-done), kind=kLoop, calls=%fused_computation.86 | loop fusion | bytes 5308416 | tf_op jit(solution)/shard_map/slice | solution.py:153
  326.9 7.1 collective-permute-start.2
  336.5 14.5 %dynamic_update_slice.39 = bf16[4,288,576]{2,0,1:T(4,128)(2,1)} dynamic-update-slice(bf16[4,288,576]{2,0,1:T(4,128)(2,1)} %get-tuple-element.191, bf16[1,288,576]{2,0,1:T(2,128)(2,1)} %copy.282, s32[]{:T(128)S(6)} %select_n.160, s32[]{:T(128)} %constant.216.clone.1, s32[]{:T(128)} %constant.216.clone.1) | dynamic-update-slice | bytes 663556 | tf_op jit(solution)/shard_map/dynamic_update_slice | solution.py:86
  353.7 14.2 %dynamic_update_slice.40 = bf16[4,288,576]{2,0,1:T(4,128)(2,1)} dynamic-update-slice(bf16[4,288,576]{2,0,1:T(4,128)(2,1)} %dynamic_update_slice.39, bf16[1,288,576]{2,0,1:T(2,128)(2,1)} %copy.283, s32[]{:T(128)S(6)} %select_n.164, s32[]{:T(128)} %constant.216.clone.1, s32[]{:T(128)} %constant.216.clone.1) | dynamic-update-slice | bytes 663556 | tf_op jit(solution)/shard_map/dynamic_update_slice | solution.py:86
  370.3 14.2 %dynamic_update_slice.41 = bf16[4,288,576]{2,0,1:T(4,128)(2,1)} dynamic-update-slice(bf16[4,288,576]{2,0,1:T(4,128)(2,1)} %dynamic_update_slice.40, bf16[1,288,576]{2,0,1:T(2,128)(2,1)} %copy.284, s32[]{:T(128)S(6)} %select_n.168, s32[]{:T(128)} %constant.216.clone.1, s32[]{:T(128)} %constant.216.clone.1) | dynamic-update-slice | bytes 663556 | tf_op jit(solution)/shard_map/dynamic_update_slice | solution.py:86
  388.8 28.4 %dynamic_update_slice.36 = bf16[4,2,288,576]{3,0,2,1:T(4,128)(2,1)S(1)} dynamic-update-slice(bf16[4,2,288,576]{3,0,2,1:T(4,128)(2,1)S(1)} %slice.112, bf16[1,2,288,576]{3,0,2,1:T(2,128)(2,1)} %copy.275, s32[]{:T(128)S(6)} %select_n.160, s32[]{:T(128)} %constant.216.clone.1, s32[]{:T(128)} %constant.216.clone.1, s32[]{:T(128)} %constant.216.clone.1) | dynamic-update-slice | bytes 1327108 | tf_op jit(solution)/shard_map/dynamic_update_slice | solution.py:86
  420.6 28.4 %dynamic_update_slice.37 = bf16[4,2,288,576]{3,0,2,1:T(4,128)(2,1)S(1)} dynamic-update-slice(bf16[4,2,288,576]{3,0,2,1:T(4,128)(2,1)S(1)} %dynamic_update_slice.36, bf16[1,2,288,576]{3,0,2,1:T(2,128)(2,1)} %copy.277, s32[]{:T(128)S(6)} %select_n.164, s32[]{:T(128)} %constant.216.clone.1, s32[]{:T(128)} %constant.216.clone.1, s32[]{:T(128)} %constant.216.clone.1) | dynamic-update-slice | bytes 1327108 | tf_op jit(solution)/shard_map/dynamic_update_slice | solution.py:86
  452.5 28.4 %dynamic_update_slice.38 = bf16[4,2,288,576]{3,0,2,1:T(4,128)(2,1)S(1)} dynamic-update-slice(bf16[4,2,288,576]{3,0,2,1:T(4,128)(2,1)S(1)} %dynamic_update_slice.37, bf16[1,2,288,576]{3,0,2,1:T(2,128)(2,1)} %copy.279, s32[]{:T(128)S(6)} %select_n.168, s32[]{:T(128)} %constant.216.clone.1, s32[]{:T(128)} %constant.216.clone.1, s32[]{:T(128)} %constant.216.clone.1) | dynamic-update-slice | bytes 1327108 | tf_op jit(solution)/shard_map/dynamic_update_slice | solution.py:86
  492.8 26.2 %collective-permute-done.3 = bf16[4,288,576]{2,0,1:T(4,128)(2,1)} collective-permute-done((bf16[4,288,576]{2,0,1:T(4,128)(2,1)}, bf16[4,288,576]{2,0,1:T(4,128)(2,1)}, u32[]{:S(2)}, u32[]{:S(2)}) %collective-permute-start.3) | collective-permute-done | bytes 1327136 | tf_op jit(solution)/shard_map/ppermute | solution.py:93
  519.0 30.4 %collective-permute-done.4 = bf16[4,288,576]{2,0,1:T(4,128)(2,1)} collective-permute-done((bf16[4,288,576]{2,0,1:T(4,128)(2,1)}, bf16[4,288,576]{2,0,1:T(4,128)(2,1)}, u32[]{:S(2)}, u32[]{:S(2)}) %collective-permute-start.4) | collective-permute-done | bytes 1327136 | tf_op jit(solution)/shard_map/ppermute | solution.py:93
  561.1 9.3 fusion.140
  570.4 8.3 multiply_convert_fusion.1
  579.9 8.0 convolution_convert_fusion
  589.2 10.9 all_to_all.69
  601.3 97.3 %reduce-scatter.6.cloned.1.call-done = bf16[96,2304]{1,0:T(8,128)(2,1)} async-done(((bf16[1536,2304]{1,0:T(8,128)(2,1)}), bf16[96,2304]{1,0:T(8,128)(2,1)}) %reduce-scatter.6.cloned.1.call-update) | async-done | bytes 442384 | tf_op jit(solution)/shard_map/reduce_scatter | solution.py:239
  703.8 65.9 %all-gather.18.cloned.1.call-done = bf16[1536,2304]{1,0:T(8,128)(2,1)} async-done(((bf16[96,2304]{1,0:T(8,128)(2,1)}), bf16[1536,2304]{1,0:T(8,128)(2,1)}) %all-gather.18.cloned.1.call-update) | async-done | bytes 7077904 | tf_op jit(solution)/shard_map/all_gather | solution.py:246
  769.7 11.4 multiply_convert_fusion
  781.1 8.9 fusion.141
  790.0 10.9 add_convert_fusion
  801.1 88.8 %reduce-scatter.8.cloned.1.call-done = bf16[96,2304]{1,0:T(8,128)(2,1)} async-done(((bf16[1536,2304]{1,0:T(8,128)(2,1)}), bf16[96,2304]{1,0:T(8,128)(2,1)}) %reduce-scatter.8.cloned.1.call-update) | async-done | bytes 442384 | tf_op jit(solution)/shard_map/reduce_scatter | solution.py:252
  897.1 6.5 fusion.48
  903.7 13.6 %all-gather.20.cloned.1.call-done = bf16[384,2304]{1,0:T(8,128)(2,1)} async-done(((bf16[96,2304]{1,0:T(8,128)(2,1)}), bf16[384,2304]{1,0:T(8,128)(2,1)}) %all-gather.20.cloned.1.call-update) | async-done | bytes 1769488 | tf_op jit(solution)/shard_map/all_gather | solution.py:270
  927.4 20.5 %fusion.20 = bf16[3072,256]{1,0:T(8,128)(2,1)} fusion(f32[3072,384,2]{1,0,2:T(8,128)} %fusion.47, f32[3072,384,2]{1,0,2:T(8,128)} %fusion.48, f32[384,2,128]{2,0,1:T(8,128)} %get-tuple-element.219, f32[384,2,128]{2,0,1:T(8,128)} %copy-done.31, f32[2,384,3072]{1,2,0:T(8,128)} %get-tuple-element.232, f32[2,384]{1,0:T(2,128)S(1)} %get-tuple-element.231), kind=kOutput, calls=%fused_computation.54 | convolution fusion | flops 1232932608 | bytes 30673920 | tf_op jit(solution)/shard_map/gqs,qgd->sd/dot_general | solution.py:280
  947.9 7.9 fusion.21
  964.1 9.6 convolution_convert_fusion.3
  980.6 8.7 convolution_convert_fusion.4
  998.1 8.6 convolution_convert_fusion.2
  1012.5 20.7 %fusion.43 = f32[384,2,256]{2,0,1:T(8,128)} fusion(f32[3072,384,2]{1,0,2:T(8,128)} %fusion.47, f32[3072,384,2]{1,0,2:T(8,128)} %fusion.48, bf16[3072,512]{1,0:T(8,128)(2,1)} %all-gather.12.cloned.1.call-done, f32[2,384,3072]{1,2,0:T(8,128)} %get-tuple-element.232, f32[2,384]{1,0:T(2,128)S(1)} %get-tuple-element.231), kind=kOutput, calls=%fused_computation.124 | convolution fusion | flops 1231752960 | bytes 49551360 | tf_op jit(solution)/shard_map/gqs,sd->qgd/dot_general | solution.py:277
  1035.5 14.5 %reduce-scatter.10.cloned.1.call-done = bf16[384,512]{1,0:T(8,128)(2,1)} async-done(((bf16[3072,512]{1,0:T(8,128)(2,1)}), bf16[384,512]{1,0:T(8,128)(2,1)}) %reduce-scatter.10.cloned.1.call-update) | async-done | bytes 393232 | tf_op jit(solution)/shard_map/reduce_scatter | solution.py:286
  1055.2 6.4 convolution_convert_fusion.1
  1070.9 28.7 %collective-permute-done.14 = bf16[4,288,576]{2,1,0:T(8,128)(2,1)} collective-permute-done((bf16[4,288,576]{2,1,0:T(8,128)(2,1)}, bf16[4,288,576]{2,1,0:T(8,128)(2,1)}, u32[]{:S(2)}, u32[]{:S(2)}) %collective-permute-start.14) | collective-permute-done | bytes 1327136 | tf_op jit(solution)/shard_map/ppermute | solution.py:104
  1104.0 35.7 %collective-permute-done.15 = bf16[1,288,576]{2,1,0:T(8,128)(2,1)S(1)} collective-permute-done((bf16[1,288,576]{2,1,0:T(8,128)(2,1)S(1)}, bf16[1,288,576]{2,1,0:T(8,128)(2,1)S(1)}, u32[]{:S(2)}, u32[]{:S(2)}) %collective-permute-start.15) | collective-permute-done | bytes 331808 | tf_op jit(solution)/shard_map/ppermute | solution.py:85
  1139.9 15.7 %collective-permute-start.16 = (bf16[1,288,576]{2,1,0:T(8,128)(2,1)S(1)}, bf16[1,288,576]{2,1,0:T(8,128)(2,1)}, u32[]{:S(2)}, u32[]{:S(2)}) collective-permute-start(bf16[1,288,576]{2,1,0:T(8,128)(2,1)S(1)} %get-tuple-element.211), channel_id=1, source_target_pairs={{0,4},{2,6},{4,0},{6,2},{1,5},{3,7},{5,1},{7,3},{8,12},{10,14},{12... | collective-permute-start | bytes 995336 | tf_op jit(solution)/shard_map/ppermute | solution.py:85
  1156.9 6.3 copy.307
  1163.1 8.1 reshape.316
  1179.6 11.2 add_multiply_fusion
  1208.8 9.0 copy.318
  1222.9 9.2 copy.320
  1232.0 6.5 copy.322
  1238.5 6.9 copy.324
  1263.4 54.4 %psum.7 = f32[4,2304]{1,0:T(4,128)S(1)} all-reduce(f32[4,2304]{1,0:T(4,128)S(1)} %pad_maximum_fusion.10), channel_id=1, replica_groups=mesh['gx'=4,'gf'=4,'gt'=2] {'gx','gf','gt'}, use_global_device_ids=true, to_apply=%region_23.24 | all-reduce | flops 9216 | bytes 73728 | tf_op jit(solution)/shard_map/psum | solution.py:316
  (342 shorter events, 257.3 us)
Async XLA Ops:
  7.2 34.9 %all-gather.10.cloned.1.call-start = ((), (), s32[]{:S(2)}) async-start(), calls=%async_computation.10 | async-start | bytes 2211840 | tf_op jit(solution)/shard_map/all_gather | solution.py:148
  7.9 106.7 %all-gather.22.cloned.1.call-start = ((), (), s32[]{:S(2)}) async-start(), calls=%async_computation.21 | async-start | bytes 5308416 | tf_op jit(solution)/shard_map/all_gather | solution.py:149
  8.7 171.9 %all-gather.12.cloned.1.call-start = ((), (), s32[]{:S(2)}) async-start(), calls=%async_computation.11 | async-start | bytes 3538944 | tf_op jit(solution)/shard_map/all_gather | solution.py:181
  41.3 78.3 %copy-start.57 = (f32[128]{0:T(128)}, f32[128]{0:T(128)S(1)}, u32[]{:S(2)}) copy-start(f32[128]{0:T(128)S(1)} %multiply_exponential_fusion) | copy-start | bytes 1540
  41.4 78.3 %copy-start.50 = (f32[384]{0:T(512)}, f32[384]{0:T(512)S(1)}, u32[]{:S(2)}) copy-start(f32[384]{0:T(512)S(1)} %fusion.99) | copy-start | bytes 4612
  42.0 77.5 %copy-start.42 = (f32[2304]{0:T(1024)}, f32[2304]{0:T(1024)S(1)}, u32[]{:S(2)}) copy-start(f32[2304]{0:T(1024)S(1)} %get-tuple-element.167) | copy-start | bytes 27652
  44.1 70.5 %copy-start.56 = (f32[384]{0:T(512)}, f32[384]{0:T(512)S(1)}, u32[]{:S(2)}) copy-start(f32[384]{0:T(512)S(1)} %add_rsqrt_fusion) | copy-start | bytes 4612
  122.0 111.1 %all-gather.14.cloned.1.call-start = ((), (), s32[]{:S(2)}) async-start(), calls=%async_computation.12 | async-start | bytes 2654208 | tf_op jit(solution)/shard_map/all_gather | solution.py:151
  127.8 769.3 %copy-start.31 = (f32[384,2,128]{2,0,1:T(8,128)}, f32[384,2,128]{2,0,1:T(8,128)S(1)}, u32[]{:S(2)}) copy-start(f32[384,2,128]{2,0,1:T(8,128)S(1)} %get-tuple-element.218) | copy-start | bytes 1179652
  237.8 25.7 %all-to-all-start = ((bf16[4,96,2304]{2,1,0:T(8,128)(2,1)}), bf16[4,96,2304]{2,1,0:T(8,128)(2,1)S(1)}, u32[]{:S(2)}, u32[]{:S(2)}) async-start(bf16[4,96,2304]{2,1,0:T(8,128)(2,1)} %bitcast.9), calls=%async_computation | async-start | bytes 3538944 | tf_op jit(solution)/shard_map/all_to_all | solution.py:224
  241.4 319.4 %all-gather.16.cloned.1.call-start = ((), (), s32[]{:S(2)}) async-start(), calls=%async_computation.13 | async-start | bytes 7520256 | tf_op jit(solution)/shard_map/all_gather | solution.py:233
  267.3 431.3 %reduce-scatter.6.cloned.1.call-start = ((), (), s32[]{:S(2)}) async-start(), calls=%async_computation.14 | async-start | bytes 7520256 | tf_op jit(solution)/shard_map/reduce_scatter | solution.py:239
  305.6 21.3 %collective-permute-start.5 = (bf16[1,288,576]{2,1,0:T(8,128)(2,1)S(1)}, bf16[1,288,576]{2,1,0:T(8,128)(2,1)}, u32[]{:S(2)}, u32[]{:S(2)}) collective-permute-start(bf16[1,288,576]{2,1,0:T(8,128)(2,1)S(1)} %bitcast.252), channel_id=1, source_target_pairs={{0,2},{2,4},{4,6},{6,0},{1,3},{3,5},{5,7},{7,1},{8,10},{10,12},{12... | collective-permute-start | bytes 995336 | tf_op jit(solution)/shard_map/ppermute | solution.py:85
  308.0 43.2 %collective-permute-start.6 = (bf16[1,288,576]{2,1,0:T(8,128)(2,1)}, bf16[1,288,576]{2,1,0:T(8,128)(2,1)}, u32[]{:S(2)}, u32[]{:S(2)}) collective-permute-start(bf16[1,288,576]{2,1,0:T(8,128)(2,1)} %bitcast.225), channel_id=1, source_target_pairs={{0,4},{2,6},{4,0},{6,2},{1,5},{3,7},{5,1},{7,3},{8,12},{10,14},{12... | collective-permute-start | bytes 995336 | tf_op jit(solution)/shard_map/ppermute | solution.py:85
  309.6 58.3 %collective-permute-start.7 = (bf16[1,288,576]{2,1,0:T(8,128)(2,1)}, bf16[1,288,576]{2,1,0:T(8,128)(2,1)}, u32[]{:S(2)}, u32[]{:S(2)}) collective-permute-start(bf16[1,288,576]{2,1,0:T(8,128)(2,1)} %bitcast.224), channel_id=1, source_target_pairs={{0,6},{2,0},{4,2},{6,4},{1,7},{3,1},{5,3},{7,5},{8,14},{10,8},{12,... | collective-permute-start | bytes 995336 | tf_op jit(solution)/shard_map/ppermute | solution.py:85
  318.7 66.8 %collective-permute-start = (bf16[1,2,288,576]{3,2,1,0:T(8,128)(2,1)}, bf16[1,2,288,576]{3,2,1,0:T(8,128)(2,1)}, u32[]{:S(2)}, u32[]{:S(2)}) collective-permute-start(bf16[1,2,288,576]{3,2,1,0:T(8,128)(2,1)} %copy.274), channel_id=1, source_target_pairs={{0,2},{2,4},{4,6},{6,0},{1,3},{3,5},{5,7},{7,1},{8,10},{10,12},{12... | collective-permute-start | bytes 1990664 | tf_op jit(solution)/shard_map/ppermute | solution.py:85
  319.6 97.6 %collective-permute-start.1 = (bf16[1,2,288,576]{3,2,1,0:T(8,128)(2,1)}, bf16[1,2,288,576]{3,2,1,0:T(8,128)(2,1)}, u32[]{:S(2)}, u32[]{:S(2)}) collective-permute-start(bf16[1,2,288,576]{3,2,1,0:T(8,128)(2,1)} %copy.276), channel_id=1, source_target_pairs={{0,4},{2,6},{4,0},{6,2},{1,5},{3,7},{5,1},{7,3},{8,12},{10,14},{12... | collective-permute-start | bytes 1990664 | tf_op jit(solution)/shard_map/ppermute | solution.py:85
  326.9 122.1 %collective-permute-start.2 = (bf16[1,2,288,576]{3,2,1,0:T(8,128)(2,1)}, bf16[1,2,288,576]{3,2,1,0:T(8,128)(2,1)}, u32[]{:S(2)}, u32[]{:S(2)}) collective-permute-start(bf16[1,2,288,576]{3,2,1,0:T(8,128)(2,1)} %copy.278), channel_id=1, source_target_pairs={{0,6},{2,0},{4,2},{6,4},{1,7},{3,1},{5,3},{7,5},{8,14},{10,8},{12,... | collective-permute-start | bytes 1990664 | tf_op jit(solution)/shard_map/ppermute | solution.py:85
  384.6 101.0 %collective-permute-start.8 = (bf16[4,288,576]{2,0,1:T(4,128)(2,1)}, bf16[4,288,576]{2,0,1:T(4,128)(2,1)}, u32[]{:S(2)}, u32[]{:S(2)}) collective-permute-start(bf16[4,288,576]{2,0,1:T(4,128)(2,1)} %dynamic_update_slice.41), channel_id=1, source_target_pairs={{0,1},{1,0},{2,3},{3,2},{4,5},{5,4},{6,7},{7,6},{8,9},{9,8},{10,11... | collective-permute-start | bytes 3981320 | tf_op jit(solution)/shard_map/ppermute | solution.py:93
  483.5 35.5 %collective-permute-start.3 = (bf16[4,288,576]{2,0,1:T(4,128)(2,1)}, bf16[4,288,576]{2,0,1:T(4,128)(2,1)}, u32[]{:S(2)}, u32[]{:S(2)}) collective-permute-start(bf16[4,288,576]{2,0,1:T(4,128)(2,1)} %get-tuple-element.203), channel_id=1, source_target_pairs={{0,1},{1,0},{2,3},{3,2},{4,5},{5,4},{6,7},{7,6},{8,9},{9,8},{10,11... | collective-permute-start | bytes 3981320 | tf_op jit(solution)/shard_map/ppermute | solution.py:93
  484.6 64.7 %collective-permute-start.4 = (bf16[4,288,576]{2,0,1:T(4,128)(2,1)}, bf16[4,288,576]{2,0,1:T(4,128)(2,1)}, u32[]{:S(2)}, u32[]{:S(2)}) collective-permute-start(bf16[4,288,576]{2,0,1:T(4,128)(2,1)} %get-tuple-element.204), channel_id=1, source_target_pairs={{0,1},{1,0},{2,3},{3,2},{4,5},{5,4},{6,7},{7,6},{8,9},{9,8},{10,11... | collective-permute-start | bytes 3981320 | tf_op jit(solution)/shard_map/ppermute | solution.py:93
  587.9 181.8 %all-gather.18.cloned.1.call-start = ((), (), s32[]{:S(2)}) async-start(), calls=%async_computation.15 | async-start | bytes 7520256 | tf_op jit(solution)/shard_map/all_gather | solution.py:246
  600.0 99.8 %copy-start.40 = (f32[2304]{0:T(1024)S(1)}, f32[2304]{0:T(1024)}, u32[]{:S(2)}) copy-start(f32[2304]{0:T(1024)} %get-tuple-element.164) | copy-start | bytes 27652
  703.8 186.1 %reduce-scatter.8.cloned.1.call-start = ((), (), s32[]{:S(2)}) async-start(), calls=%async_computation.16 | async-start | bytes 7520256 | tf_op jit(solution)/shard_map/reduce_scatter | solution.py:252
  801.0 88.9 %copy-start.5 = (f32[96,2304]{1,0:T(8,128)S(1)}, f32[96,2304]{1,0:T(8,128)}, u32[]{:S(2)}) copy-start(f32[96,2304]{1,0:T(8,128)} %copy-done.4) | copy-start | bytes 2654212
  801.0 90.7 %copy-start.3 = (f32[96,2304]{1,0:T(8,128)S(1)}, f32[96,2304]{1,0:T(8,128)}, u32[]{:S(2)}) copy-start(f32[96,2304]{1,0:T(8,128)} %copy-done.2) | copy-start | bytes 2654212
  801.0 90.7 %copy-start.13 = (bf16[96,2304]{1,0:T(8,128)(2,1)S(1)}, bf16[96,2304]{1,0:T(8,128)(2,1)}, u32[]{:S(2)}) copy-start(bf16[96,2304]{1,0:T(8,128)(2,1)} %reduce-scatter.6.cloned.1.call-done) | copy-start | bytes 1327108
  801.0 116.2 %all-gather.20.cloned.1.call-start = ((), (), s32[]{:S(2)}) async-start(), calls=%async_computation.17 | async-start | bytes 2211840 | tf_op jit(solution)/shard_map/all_gather | solution.py:270
  896.7 153.3 %reduce-scatter.10.cloned.1.call-start = ((), (), s32[]{:S(2)}) async-start(), calls=%async_computation.18 | async-start | bytes 3538944 | tf_op jit(solution)/shard_map/reduce_scatter | solution.py:286
  959.6 301.1 %reduce-scatter.14.cloned.1.call-start = ((), (), s32[]{:S(2)}) async-start(), calls=%async_computation.20 | async-start | bytes 2654208 | tf_op jit(solution)/shard_map/reduce_scatter | solution.py:313
  964.1 355.7 %reduce-scatter.12.cloned.1.call-start = ((), (), s32[]{:S(2)}) async-start(), calls=%async_computation.19 | async-start | bytes 5308416 | tf_op jit(solution)/shard_map/reduce_scatter | solution.py:310
  979.1 82.6 %collective-permute-start.10 = (bf16[4,288,576]{2,1,0:T(8,128)(2,1)}, bf16[4,288,576]{2,1,0:T(8,128)(2,1)}, u32[]{:S(2)}, u32[]{:S(2)}) collective-permute-start(bf16[4,288,576]{2,1,0:T(8,128)(2,1)} %dynamic-slice_bitcast_fusion.1), channel_id=1, source_target_pairs={{0,1},{1,0},{2,3},{3,2},{4,5},{5,4},{6,7},{7,6},{8,9},{9,8},{10,11... | collective-permute-start | bytes 3981320 | tf_op jit(solution)/shard_map/ppermute | solution.py:104
  996.6 67.4 %collective-permute-start.9 = (bf16[4,288,576]{2,1,0:T(8,128)(2,1)}, bf16[4,288,576]{2,1,0:T(8,128)(2,1)}, u32[]{:S(2)}, u32[]{:S(2)}) collective-permute-start(bf16[4,288,576]{2,1,0:T(8,128)(2,1)} %dynamic-slice_bitcast_fusion.2), channel_id=1, source_target_pairs={{0,1},{1,0},{2,3},{3,2},{4,5},{5,4},{6,7},{7,6},{8,9},{9,8},{10,11... | collective-permute-start | bytes 3981320 | tf_op jit(solution)/shard_map/ppermute | solution.py:104
  1012.0 87.6 %collective-permute-start.14 = (bf16[4,288,576]{2,1,0:T(8,128)(2,1)}, bf16[4,288,576]{2,1,0:T(8,128)(2,1)}, u32[]{:S(2)}, u32[]{:S(2)}) collective-permute-start(bf16[4,288,576]{2,1,0:T(8,128)(2,1)} %dynamic-slice_bitcast_fusion), channel_id=1, source_target_pairs={{0,1},{1,0},{2,3},{3,2},{4,5},{5,4},{6,7},{7,6},{8,9},{9,8},{10,11... | collective-permute-start | bytes 3981320 | tf_op jit(solution)/shard_map/ppermute | solution.py:104
  1066.4 36.5 %copy-start.58 = (f32[96]{0:T(128)S(1)}, f32[96]{0:T(128)}, u32[]{:S(2)}) copy-start(f32[96]{0:T(128)} %get-tuple-element.225) | copy-start | bytes 1156
  1066.4 36.5 %copy-start.48 = (f32[2304]{0:T(1024)S(1)}, f32[2304]{0:T(1024)}, u32[]{:S(2)}) copy-start(f32[2304]{0:T(1024)} %get-tuple-element.162) | copy-start | bytes 27652
  1066.4 89.6 %collective-permute-start.11 = (bf16[1,2,288,576]{3,2,0,1:T(8,128)(2,1)S(1)}, bf16[1,2,288,576]{3,2,0,1:T(8,128)(2,1)S(1)}, u32[]{:S(2)}, u32[]{:S(2)}) collective-permute-start(bf16[1,2,288,576]{3,2,0,1:T(8,128)(2,1)S(1)} %get-tuple-element.197), channel_id=1, source_target_pairs={{0,2},{2,4},{4,6},{6,0},{1,3},{3,5},{5,7},{7,1},{8,10},{10,12},{12... | collective-permute-start | bytes 1990664 | tf_op jit(solution)/shard_map/ppermute | solution.py:85
  1067.5 88.7 %collective-permute-start.12 = (bf16[1,2,288,576]{3,2,0,1:T(8,128)(2,1)S(1)}, bf16[1,2,288,576]{3,2,0,1:T(8,128)(2,1)S(1)}, u32[]{:S(2)}, u32[]{:S(2)}) collective-permute-start(bf16[1,2,288,576]{3,2,0,1:T(8,128)(2,1)S(1)} %get-tuple-element.198), channel_id=1, source_target_pairs={{0,4},{2,6},{4,0},{6,2},{1,5},{3,7},{5,1},{7,3},{8,12},{10,14},{12... | collective-permute-start | bytes 1990664 | tf_op jit(solution)/shard_map/ppermute | solution.py:85
  1068.8 87.6 %collective-permute-start.13 = (bf16[1,2,288,576]{3,2,0,1:T(8,128)(2,1)S(1)}, bf16[1,2,288,576]{3,2,0,1:T(8,128)(2,1)S(1)}, u32[]{:S(2)}, u32[]{:S(2)}) collective-permute-start(bf16[1,2,288,576]{3,2,0,1:T(8,128)(2,1)S(1)} %get-tuple-element.196), channel_id=1, source_target_pairs={{0,6},{2,0},{4,2},{6,4},{1,7},{3,1},{5,3},{7,5},{8,14},{10,8},{12,... | collective-permute-start | bytes 1990664 | tf_op jit(solution)/shard_map/ppermute | solution.py:85
  1101.4 38.3 %collective-permute-start.15 = (bf16[1,288,576]{2,1,0:T(8,128)(2,1)S(1)}, bf16[1,288,576]{2,1,0:T(8,128)(2,1)S(1)}, u32[]{:S(2)}, u32[]{:S(2)}) collective-permute-start(bf16[1,288,576]{2,1,0:T(8,128)(2,1)S(1)} %constant_dynamic-slice_fusion.3), channel_id=1, source_target_pairs={{0,2},{2,4},{4,6},{6,0},{1,3},{3,5},{5,7},{7,1},{8,10},{10,12},{12... | collective-permute-start | bytes 995336 | tf_op jit(solution)/shard_map/ppermute | solution.py:85
  1139.9 35.8 %collective-permute-start.16 = (bf16[1,288,576]{2,1,0:T(8,128)(2,1)S(1)}, bf16[1,288,576]{2,1,0:T(8,128)(2,1)}, u32[]{:S(2)}, u32[]{:S(2)}) collective-permute-start(bf16[1,288,576]{2,1,0:T(8,128)(2,1)S(1)} %get-tuple-element.211), channel_id=1, source_target_pairs={{0,4},{2,6},{4,0},{6,2},{1,5},{3,7},{5,1},{7,3},{8,12},{10,14},{12... | collective-permute-start | bytes 995336 | tf_op jit(solution)/shard_map/ppermute | solution.py:85
  1155.6 22.2 %collective-permute-start.17 = (bf16[1,288,576]{2,1,0:T(8,128)(2,1)S(1)}, bf16[1,288,576]{2,1,0:T(8,128)(2,1)}, u32[]{:S(2)}, u32[]{:S(2)}) collective-permute-start(bf16[1,288,576]{2,1,0:T(8,128)(2,1)S(1)} %get-tuple-element.210), channel_id=1, source_target_pairs={{0,6},{2,0},{4,2},{6,4},{1,7},{3,1},{5,3},{7,5},{8,14},{10,8},{12,... | collective-permute-start | bytes 995336 | tf_op jit(solution)/shard_map/ppermute | solution.py:85
  1192.3 11.9 all-to-all-start.1
  1204.2 48.6 %all-to-all-start.3 = ((bf16[4,96,2304]{2,1,0:T(8,128)(2,1)}), bf16[4,96,2304]{2,1,0:T(8,128)(2,1)}, u32[]{:S(2)}, u32[]{:S(2)}) async-start(bf16[4,96,2304]{2,1,0:T(8,128)(2,1)} %bitcast.247), calls=%async_computation.6 | async-start | bytes 3538944 | tf_op jit(solution)/shard_map/all_to_all | solution.py:224
  1257.1 60.7 %copy-start.53 = (bf16[4,288]{1,0:T(4,128)(2,1)S(1)}, bf16[4,288]{1,0:T(4,128)(2,1)}, u32[]{:S(2)}) copy-start(bf16[4,288]{1,0:T(4,128)(2,1)} %param.25) | copy-start | bytes 6916
  1257.1 60.7 %copy-start.54 = (f32[4,288]{1,0:T(4,128)S(1)}, f32[4,288]{1,0:T(4,128)}, u32[]{:S(2)}) copy-start(f32[4,288]{1,0:T(4,128)} %param.35) | copy-start | bytes 13828
  1257.1 60.7 %copy-start.55 = (f32[4,288]{1,0:T(4,128)S(1)}, f32[4,288]{1,0:T(4,128)}, u32[]{:S(2)}) copy-start(f32[4,288]{1,0:T(4,128)} %param.30) | copy-start | bytes 13828
  1257.1 61.4 %all-to-all-start.4 = ((f32[96,4,576]{2,0,1:T(8,128)}), f32[96,4,576]{2,0,1:T(8,128)S(1)}, u32[]{:S(2)}, u32[]{:S(2)}) async-start(f32[96,4,576]{2,0,1:T(8,128)} %copy.303), calls=%async_computation.7 | async-start | bytes 1966080 | tf_op jit(solution)/shard_map/all_to_all | solution.py:308
  (58 other events, 487.8 us)
Sparse Core Ops, SparseCore 0:
  9.6 23.4 all-gather.9
  35.2 79.3 all-gather.21
  122.1 58.3 all-gather.11
  182.6 50.4 all-gather.13
  267.4 85.9 all-gather.15
  588.0 110.5 reduce-scatter.5
  703.9 65.7 all-gather.17
  801.1 88.6 reduce-scatter.7
  896.8 20.4 all-gather.19
  959.8 90.1 reduce-scatter.9
  1053.5 133.5 reduce-scatter.13
  1190.5 96.4 reduce-scatter.11
